TPU v7x, 32 devices: a whole 2x2x4 slice. The times are simulated.
32 devices in a mesh: depth: 4 (over z), wide: 8 (over y, x, core).
Axes of the slice: x: 2, y: 2, z: 4, core: 2. Of those that a mesh axis runs over, the one named last changes fastest.
Arguments:
- density: float32 [4, 4096, 4096], P('depth', 'wide'), may hold values from -4 to 4
- layer_top: float32 [4], P('depth'), may hold values from 0.75 to 1.5
- layer_thick: float32 [4], P('depth'), may hold values from 1.5 to 3
- sample_row: int32 [32, 256], P(('depth', 'wide')), may hold values from 0 to 127
- sample_col: int32 [32, 256], P(('depth', 'wide')), may hold values from 0 to 4095
- sample_frac: int32 [32, 2, 256], P(('depth', 'wide')), may hold values from 0 to 15
- sample_owner: int32 [32, 256, 1], P(('depth', 'wide')), may hold values from 0 to 7; in each aligned block of 256 rows (0 to 255, 256 to 511, ..., all dimensions but the last counted through in order) at most 64 rows name the same one
Outputs:
- gradient_grid: float32 [6, 4096, 4096], P(None, ('depth', 'wide'))
- line_samples: float32 [6, 32, 512], P(None, ('depth', 'wide'))
Inputs may be any that keep to these rules, and one draw needn't show every extreme that they name: `sample_owner`: among the 256 samples of one tile no owner is named more than 64 times, a bound that some block reaches.
All inputs are finite; a program needn't handle non-finite values.
Results may differ from a plain program's by a relative error of at most 0.0001.
Values sent between devices are 32-bit elements; how exact they have to be, the bound alone decides.
No kernel may reach another device: no remote copies, remote signals or barrier semaphores. Data moves between devices by JAX's collectives and lax.ppermute only.
A program may use at most 320 MiB of HBM per device.

v0:
```python
import math

import jax
import jax.numpy as jnp
from jax import lax
from jax.sharding import PartitionSpec as P

RADIX = 128
QLEV = 16


HIGH = lax.Precision.HIGHEST


def padded_2(block, sides, width):
    for axis, dim in sides:
        count = lax.axis_size(axis)
        forward = [(i, i + 1) for i in range(count - 1)]
        forward.append((count - 1, 0))
        backward = [(target, source) for source, target in forward]
        low = lax.ppermute(
            lax.slice_in_dim(block, block.shape[dim] - width, None, axis=dim), axis, forward
        )
        high = lax.ppermute(lax.slice_in_dim(block, 0, width, axis=dim), axis, backward)
        block = jnp.concatenate([low, block, high], axis=dim)
    return block


def product(formula, operand_a, operand_b):
    return jnp.einsum(formula, operand_a, operand_b, precision=HIGH)


def complex_product(formula, complex_pair, table_pair):
    real_part = product(formula, complex_pair[0], table_pair[0]) - product(
        formula, complex_pair[1], table_pair[1]
    )
    imag_part = product(formula, complex_pair[0], table_pair[1]) + product(
        formula, complex_pair[1], table_pair[0]
    )
    return (real_part, imag_part)


def phase_table(row_count, col_count, period, orient):
    left_ids = jnp.arange(row_count, dtype=jnp.int32)[:, None]
    right_ids = jnp.arange(col_count, dtype=jnp.int32)[None, :]
    angles = (left_ids * right_ids % period).astype(jnp.float32) * (2.0 * math.pi / period)
    return (jnp.cos(angles), orient * jnp.sin(angles))


def times_table(complex_pair, table_pair):
    return (
        complex_pair[0] * table_pair[0] - complex_pair[1] * table_pair[1],
        complex_pair[0] * table_pair[1] + complex_pair[1] * table_pair[0],
    )


def column_forward(complex_pair):
    grid_len = complex_pair[0].shape[0]
    outer_len = grid_len // RADIX
    item_count = complex_pair[0].shape[2]
    columns = (
        complex_pair[0].reshape(outer_len, RADIX, item_count),
        complex_pair[1].reshape(outer_len, RADIX, item_count),
    )
    partial_value = complex_product(
        "bcd,ab->acd", columns, phase_table(outer_len, outer_len, outer_len, -1.0)
    )
    twiddles = phase_table(outer_len, RADIX, grid_len, -1.0)
    partial_value = times_table(partial_value, (twiddles[0][:, :, None], twiddles[1][:, :, None]))
    return complex_product("abd,bc->acd", partial_value, phase_table(RADIX, RADIX, RADIX, -1.0))


def row_inverse(complex_pair):
    dims_in = complex_pair[0].shape
    grid_len = dims_in[-1]
    outer_len = grid_len // RADIX
    flat_dims = (-1, outer_len, RADIX)
    row_values = (complex_pair[0].reshape(flat_dims), complex_pair[1].reshape(flat_dims))
    partial_value = complex_product(
        "zab,cb->zac", row_values, phase_table(RADIX, RADIX, RADIX, 1.0)
    )
    partial_value = times_table(partial_value, phase_table(outer_len, RADIX, grid_len, 1.0))
    partial_value = complex_product(
        "zbc,ab->zac", partial_value, phase_table(outer_len, outer_len, outer_len, 1.0)
    )
    return (partial_value[0].reshape(dims_in), partial_value[1].reshape(dims_in))


def column_inverse_start(complex_pair):
    outer_len = complex_pair[0].shape[1]
    partial_value = complex_product(
        "jabd,cb->jacd", complex_pair, phase_table(RADIX, RADIX, RADIX, 1.0)
    )
    twiddles = phase_table(outer_len, RADIX, outer_len * RADIX, 1.0)
    return times_table(partial_value, (twiddles[0][:, :, None], twiddles[1][:, :, None]))


def wavenumber(wave_index, grid_len):
    signed_ids = jnp.where(wave_index < grid_len // 2, wave_index, wave_index - grid_len).astype(
        jnp.float32
    )
    full_wave = signed_ids * (2.0 * math.pi / grid_len)
    odd_wave = jnp.where(wave_index == grid_len // 2, 0.0, full_wave)
    return (full_wave, odd_wave)


def channel_spectra(continued, full_x, full_y, odd_x, odd_y, safe_square, safe_root):
    real_part, imag_part = continued
    coef_xx = -full_x * full_x / safe_square
    coef_yy = -full_y * full_y / safe_square
    coef_xy = -odd_x * odd_y / safe_square
    slope_x = odd_x / safe_root
    slope_y = odd_y / safe_root
    first_pair = (
        real_part * coef_xx - imag_part * coef_yy,
        real_part * coef_yy + imag_part * coef_xx,
    )
    second_pair = (real_part * coef_xy - imag_part, real_part + imag_part * coef_xy)
    third_pair = (
        -real_part * slope_y - imag_part * slope_x,
        real_part * slope_x - imag_part * slope_y,
    )
    return (
        jnp.stack([first_pair[0], second_pair[0], third_pair[0]]),
        jnp.stack([first_pair[1], second_pair[1], third_pair[1]]),
    )


def ordered_channels(real_fields, imag_fields):
    return jnp.concatenate(
        [real_fields, imag_fields[0:1], imag_fields[2:3], imag_fields[1:2]], axis=0
    )


def cubic_kernel(distance):
    near_part = (1.5 * distance - 2.5) * distance * distance + 1.0
    far_part = ((-0.5 * distance + 2.5) * distance - 4.0) * distance + 2.0
    return jnp.where(distance <= 1.0, near_part, jnp.where(distance < 2.0, far_part, 0.0))


def weight_rows(levels):
    level_ids = jnp.arange(levels, dtype=jnp.int32)
    offsets = (level_ids.astype(jnp.float32) + 0.5) / levels - 0.5
    bases = jnp.where(level_ids < levels // 2, -1.0, 0.0).astype(jnp.float32)
    fraction = offsets - bases
    tap_pos = jnp.arange(4, dtype=jnp.int32).astype(jnp.float32) - 1.0
    return cubic_kernel(jnp.abs(fraction[:, None] - tap_pos[None, :]))


def per_device(density, layer_top, layer_thick, sample_row, sample_col, sample_frac, sample_owner):
    wide_count = lax.axis_size("wide")
    depth_count = lax.axis_size("depth")
    rows_here = density.shape[1]
    grid_len = density.shape[2]
    outer_len = grid_len // RADIX
    local_cols = grid_len // wide_count
    tile_rows = rows_here // depth_count
    layer_field = density[0].reshape(rows_here, outer_len, RADIX)
    first_table = phase_table(outer_len, outer_len, outer_len, -1.0)
    partial_value = (
        product("rbc,ab->rac", layer_field, first_table[0]),
        product("rbc,ab->rac", layer_field, first_table[1]),
    )
    partial_value = times_table(partial_value, phase_table(outer_len, RADIX, grid_len, -1.0))
    partial_value = complex_product(
        "rab,bc->rac", partial_value, phase_table(RADIX, RADIX, RADIX, -1.0)
    )
    row_spectra = (
        partial_value[0].reshape(rows_here, wide_count, local_cols),
        partial_value[1].reshape(rows_here, wide_count, local_cols),
    )
    spectrum = column_forward(
        (
            lax.all_to_all(row_spectra[0], "wide", split_axis=1, concat_axis=0, tiled=True),
            lax.all_to_all(row_spectra[1], "wide", split_axis=1, concat_axis=0, tiled=True),
        )
    )
    position = lax.axis_index("wide") * local_cols + jnp.arange(local_cols, dtype=jnp.int32)
    index_x = position // RADIX + outer_len * (position % RADIX)
    index_y = (
        jnp.arange(outer_len, dtype=jnp.int32)[:, None]
        + outer_len * jnp.arange(RADIX, dtype=jnp.int32)[None, :]
    )
    full_x, odd_x = wavenumber(index_x, grid_len)
    full_y, odd_y = wavenumber(index_y, grid_len)
    full_x = full_x[None, None, :]
    odd_x = odd_x[None, None, :]
    full_y = full_y[:, :, None]
    odd_y = odd_y[:, :, None]
    squared = full_x * full_x + full_y * full_y
    magnitude = jnp.sqrt(squared)
    safe_square = jnp.where(squared > 0.0, squared, 1.0)
    safe_root = jnp.sqrt(safe_square)
    continuation = (
        2.0
        * math.pi
        / (grid_len * grid_len)
        * (1.0 - jnp.exp(-magnitude * layer_thick[0]))
        * jnp.exp(-magnitude * layer_top[0])
    )
    continued = (spectrum[0] * continuation, spectrum[1] * continuation)
    summed = lax.psum((continued[0], continued[1]), "depth")
    channels = channel_spectra(summed, full_x, full_y, odd_x, odd_y, safe_square, safe_root)
    partial_value = column_inverse_start(channels)
    row_share = outer_len // depth_count
    row_start = lax.axis_index("depth") * row_share
    back_table = phase_table(outer_len, outer_len, outer_len, 1.0)
    share_table = (
        lax.dynamic_slice_in_dim(back_table[0], row_start, row_share, 0),
        lax.dynamic_slice_in_dim(back_table[1], row_start, row_share, 0),
    )
    partial_value = complex_product("jbcd,ab->jacd", partial_value, share_table)
    row_blocks = (
        partial_value[0].reshape(3, wide_count, tile_rows, local_cols),
        partial_value[1].reshape(3, wide_count, tile_rows, local_cols),
    )
    row_fields = row_inverse(
        (
            lax.all_to_all(row_blocks[0], "wide", split_axis=1, concat_axis=3, tiled=True),
            lax.all_to_all(row_blocks[1], "wide", split_axis=1, concat_axis=3, tiled=True),
        )
    )
    gradient = ordered_channels(row_fields[0], row_fields[1]).reshape(6, tile_rows, grid_len)
    padded = padded_2(gradient, ((("depth", "wide"), 1),), 2)
    weight_table = weight_rows(QLEV)
    level_ids = jnp.arange(QLEV, dtype=jnp.int32)[None, :]
    frac_y = sample_frac[0, 0]
    frac_x = sample_frac[0, 1]
    weight_y = jnp.dot(
        (frac_y[:, None] == level_ids).astype(jnp.float32), weight_table, precision=HIGH
    )
    weight_x = jnp.dot(
        (frac_x[:, None] == level_ids).astype(jnp.float32), weight_table, precision=HIGH
    )
    base_y = jnp.where(frac_y < QLEV // 2, -1, 0).astype(jnp.int32)
    base_x = jnp.where(frac_x < QLEV // 2, -1, 0).astype(jnp.int32)
    tap_ids = jnp.arange(4, dtype=jnp.int32)[None, :]
    row_ids = (sample_row[0] + base_y + 1)[:, None] + tap_ids
    col_ids = ((sample_col[0] + base_x - 1)[:, None] + tap_ids) % grid_len
    neighbours = padded[:, row_ids[:, :, None], col_ids[:, None, :]]
    interpolated = jnp.einsum("csab,sa,sb->cs", neighbours, weight_y, weight_x, precision=HIGH)
    sample_count = sample_row.shape[1]
    capacity = max(2 * sample_count // wide_count, 2)
    slot_total = wide_count * capacity
    owner_ids = sample_owner[0, :, 0]
    owner_marks = (owner_ids[:, None] == jnp.arange(wide_count, dtype=jnp.int32)[None, :]).astype(
        jnp.int32
    )
    earlier = jnp.cumsum(owner_marks, axis=0) - owner_marks
    slot_ids = jnp.sum(earlier * owner_marks, axis=1)
    target = owner_ids * capacity + slot_ids
    placement = (target[:, None] == jnp.arange(slot_total, dtype=jnp.int32)[None, :]).astype(
        jnp.float32
    )
    outgoing = jnp.dot(interpolated, placement, precision=HIGH).reshape(6, wide_count, capacity)
    arrived = lax.all_to_all(outgoing, "wide", split_axis=1, concat_axis=1, tiled=True)
    return (gradient, arrived.reshape(6, 1, slot_total))


def solution(mesh):
    in_specs = (
        P("depth", "wide", None),
        P("depth"),
        P("depth"),
        P(("depth", "wide"), None),
        P(("depth", "wide"), None),
        P(("depth", "wide"), None, None),
        P(("depth", "wide"), None, None),
    )
    out_specs = (P(None, ("depth", "wide"), None), P(None, ("depth", "wide"), None))
    return jax.shard_map(
        per_device, mesh=mesh, in_specs=in_specs, out_specs=out_specs, check_vma=False
    )
```

profile of v0, /device:TPU:0, one launch (start us, length us, event | category | flops | bytes accessed | tf_op | source)
XLA Modules:
  0.0 1574.5 jit_solution(17820646528729374179)
XLA Ops:
  79.8 18.6 %fusion.46 = f32[512,32,128]{0,2,1:T(8,128)S(1)} fusion(f32[512,32,128]{2,1,0:T(8,128)} %copy-done.5), kind=kOutput, calls=%fused_computation.69 | convolution fusion | flops 3221471232 | bytes 16777216 | tf_op jit(solution)/shard_map/rab,bc->rac/dot_general | solution.py:30
  98.5 21.9 %fusion.68 = f32[512,32,128]{0,2,1:T(8,128)} fusion(f32[512,32,128]{0,2,1:T(8,128)S(1)} %fusion.46, f32[512,32,128]{2,1,0:T(8,128)} %copy-done.2), kind=kOutput, calls=%fused_computation.97 | convolution fusion | flops 3223552000 | bytes 25165824 | tf_op jit(solution)/shard_map/rab,bc->rac/dot_general | solution.py:30
  129.4 44.9 %all-to-all-done.1 = f32[512,8,512]{2,0,1:T(8,128)} async-done(((f32[512,8,512]{2,0,1:T(8,128)}), f32[512,8,512]{2,0,1:T(8,128)}, u32[]{:S(2)}, u32[]{:S(2)}) %all-to-all-start.1) | async-done | bytes 8388640 | tf_op jit(solution)/shard_map/all_to_all | solution.py:175
  180.9 17.1 %fusion.36 = f32[32,128,512]{2,0,1:T(8,128)} fusion(f32[32,128,512]{2,1,0:T(8,128)} %bitcast.22), kind=kOutput, calls=%fused_computation.59 | convolution fusion | flops 805320704 | bytes 16777216 | tf_op jit(solution)/shard_map/bcd,ab->acd/dot_general | solution.py:30
  198.0 17.6 %fusion.38 = f32[32,128,512]{2,0,1:T(8,128)} fusion(f32[32,128,512]{2,1,0:T(8,128)} %bitcast.22), kind=kOutput, calls=%fused_computation.61 | convolution fusion | flops 805321728 | bytes 16777216 | tf_op jit(solution)/shard_map/bcd,ab->acd/dot_general | solution.py:30
  215.7 57.7 %all-to-all-done = f32[512,8,512]{2,0,1:T(8,128)} async-done(((f32[512,8,512]{2,0,1:T(8,128)}), f32[512,8,512]{2,0,1:T(8,128)}, u32[]{:S(2)}, u32[]{:S(2)}) %all-to-all-start) | async-done | bytes 8388640 | tf_op jit(solution)/shard_map/all_to_all | solution.py:174
  273.4 17.5 %fusion.42 = f32[32,128,512]{2,0,1:T(8,128)} fusion(f32[32,128,512]{2,1,0:T(8,128)} %bitcast.16), kind=kOutput, calls=%fused_computation.65 | convolution fusion | flops 805320704 | bytes 16777216 | tf_op jit(solution)/shard_map/bcd,ab->acd/dot_general | solution.py:30
  290.9 24.4 %multiply_subtract_fusion = (f32[32,128,512]{2,0,1:T(8,128)}, f32[32,128,512]{2,0,1:T(8,128)}) fusion(f32[32,128]{0,1:T(8,128)S(1)} %copy.142, f32[32,128]{0,1:T(8,128)S(1)} %copy.139, f32[32,128,512]{2,0,1:T(8,128)} %fusion.36, f32[32,128,512]{2,0,1:T(8,128)} %fusion.42, f32[32,128,512]{2,0,1:T(8,128)} %fusion.38, f32[32,128,512]{2,1,0:T(8,128)} %bitcast.16), kind=kOutput, calls=%fused_computation.48 | convolution fusion | flops 822098944 | bytes 50364416 | tf_op jit(solution)/shard_map/bcd,ab->acd/dot_general | solution.py:30
  315.3 18.1 %fusion.28 = f32[128,32,512]{2,0,1:T(8,128)S(1)} fusion(f32[32,128,512]{2,0,1:T(8,128)} %get-tuple-element.15), kind=kOutput, calls=%fused_computation.51 | convolution fusion | flops 3221454848 | bytes 16777216 | tf_op jit(solution)/shard_map/abd,bc->acd/dot_general | solution.py:30
  345.8 18.2 %bitcast_multiply_fusion.5 = f32[32,128,512]{2,1,0:T(8,128)} fusion(f32[128,32,512]{2,0,1:T(8,128)S(1)} %fusion.30, f32[]{:T(128)} %bitcast.208, f32[]{:T(128)} %bitcast.210, f32[32,128]{1,0:T(8,128)S(1)} %get-tuple-element.40, f32[512]{0:T(512)S(1)} %fusion.224, f32[32,128,512]{2,0,1:T(8,128)S(1)} %bitcast.220), kind=kOutput, calls=%fused_computation.40 | convolution fusion | flops 3240329216 | bytes 25184264 | tf_op jit(solution)/shard_map/abd,bc->acd/dot_general | solution.py:30
  364.0 18.5 %bitcast_multiply_fusion.4 = f32[32,128,512]{2,1,0:T(8,128)} fusion(f32[128,32,512]{2,0,1:T(8,128)S(1)} %fusion.28, f32[]{:T(128)} %bitcast.209, f32[]{:T(128)} %bitcast.211, f32[32,128]{1,0:T(8,128)S(1)} %get-tuple-element.40, f32[512]{0:T(512)S(1)} %fusion.224, f32[32,128,512]{2,0,1:T(8,128)S(1)} %bitcast.220), kind=kOutput, calls=%fused_computation.39 | convolution fusion | flops 3240345600 | bytes 25184264 | tf_op jit(solution)/shard_map/abd,bc->acd/dot_general | solution.py:30
  382.8 563.3 %all-reduce.3.cloned.1.call-done = (f32[32,128,512]{2,1,0:T(8,128)}, f32[32,128,512]{2,1,0:T(8,128)}) async-done(((f32[32,128,512]{2,1,0:T(8,128)}, f32[32,128,512]{2,1,0:T(8,128)}), (f32[32,128,512]{2,1,0:T(8,128)}, f32[32,128,512]{2,1,0:T(8,128)})) %all-reduce.3.cloned.1.call-update) | async-done | bytes 16777232 | tf_op jit(solution)/shard_map/psum | solution.py:202
  946.1 21.0 %add_bitcast_fusion.1 = (f32[1,32,128,512]{3,2,1,0:T(8,128)}, f32[1,32,128,512]{3,2,1,0:T(8,128)S(1)}, f32[1,32,128,512]{3,2,1,0:T(8,128)}, f32[1,32,128,512]{3,...) fusion(f32[32,128,512]{2,1,0:T(8,128)} %get-tuple-element.10, ...), kind=kLoop, calls=%fused_computation.43 | loop fusion | flops 54525952 | bytes 67166208 | tf_op jit(solution)/shard_map/stack | solution.py:125
  967.1 34.1 %fusion.10 = f32[128,3,32,512]{3,0,2,1:T(8,128)} fusion(f32[1,32,128,512]{3,2,1,0:T(8,128)} %get-tuple-element.28, f32[1,32,128,512]{3,2,1,0:T(8,128)} %get-tuple-element.31, f32[1,32,128,512]{3,2,1,0:T(8,128)} %get-tuple-element.18), kind=kOutput, calls=%fused_computation.18 | convolution fusion | flops 9676488704 | bytes 50331648 | tf_op jit(solution)/shard_map/jabd,cb->jacd/dot_general | solution.py:30
  1001.2 29.1 %fusion.11 = f32[128,3,32,512]{3,0,2,1:T(8,128)} fusion(f32[1,32,128,512]{3,2,1,0:T(8,128)} %get-tuple-element.28, f32[1,32,128,512]{3,2,1,0:T(8,128)} %get-tuple-element.31, f32[1,32,128,512]{3,2,1,0:T(8,128)} %get-tuple-element.18), kind=kOutput, calls=%fused_computation.19 | convolution fusion | flops 9676488704 | bytes 50331648 | tf_op jit(solution)/shard_map/jabd,cb->jacd/dot_general | solution.py:30
  1030.4 28.4 %fusion.13 = f32[128,3,32,512]{3,0,2,1:T(8,128)} fusion(f32[1,32,128,512]{3,2,1,0:T(8,128)S(1)} %get-tuple-element.29, f32[1,32,128,512]{3,2,1,0:T(8,128)} %get-tuple-element.30, f32[1,32,128,512]{3,2,1,0:T(8,128)S(1)} %get-tuple-element.19), kind=kOutput, calls=%fused_computation.21 | convolution fusion | flops 9676488704 | bytes 50331648 | tf_op jit(solution)/shard_map/jabd,cb->jacd/dot_general | solution.py:30
  1058.8 60.9 %fusion = (f32[3,32,128,512]{3,2,1,0:T(8,128)}, f32[3,32,128,512]{3,2,1,0:T(8,128)}) fusion(f32[32,128]{1,0:T(8,128)S(1)} %fusion.189, f32[32,128]{1,0:T(8,128)S(1)} %get-tuple-element.43, f32[128,3,32,512]{3,0,2,1:T(8,128)} %fusion.10, f32[128,3,32,512]{3,0,2,1:T(8,128)} %fusion.13, f32[128,3,32,512]{3,0,2,1:T(8,128)} %fusion.11, ...), kind=kOutput, calls=%fused_computation.5 | convolution fusion | flops 9726820352 | bytes 151027712 | tf_op jit(solution)/shard_map/jabd,cb->jacd/dot_general | solution.py:30
  1119.6 34.6 %fusion.2 = f32[8,3,128,512]{3,0,2,1:T(8,128)} fusion(f32[3,32,128,512]{3,2,1,0:T(8,128)} %get-tuple-element.13, f32[32,32]{1,0:T(8,128)S(1)} %fusion.192, s32[]{:T(128)S(6)} %select_n.307), kind=kOutput, calls=%fused_computation.10 | convolution fusion | flops 603979776 | bytes 31461380 | tf_op jit(solution)/shard_map/jbcd,ab->jacd/dot_general | solution.py:30
  1154.2 26.1 %add_bitcast_fusion.4 = f32[3,8,128,512]{3,1,2,0:T(8,128)S(1)} fusion(f32[8,3,128,512]{3,0,2,1:T(8,128)} %fusion.2, f32[3,32,128,512]{3,2,1,0:T(8,128)S(1)} %copy-done, f32[32,32]{1,0:T(8,128)S(1)} %fusion.191, s32[]{:T(128)S(6)} %select_n.307), kind=kOutput, calls=%fused_computation.79 | convolution fusion | flops 605552640 | bytes 37752836 | tf_op jit(solution)/shard_map/jbcd,ab->jacd/dot_general | solution.py:30
  1191.5 33.3 %fusion.4 = f32[8,3,128,512]{3,0,2,1:T(8,128)S(1)} fusion(f32[3,32,128,512]{3,2,1,0:T(8,128)} %get-tuple-element.13, f32[32,32]{1,0:T(8,128)S(1)} %fusion.191, s32[]{:T(128)S(6)} %select_n.307), kind=kOutput, calls=%fused_computation.12 | convolution fusion | flops 603979776 | bytes 31461380 | tf_op jit(solution)/shard_map/jbcd,ab->jacd/dot_general | solution.py:30
  1224.8 33.7 %subtract_bitcast_fusion.6 = f32[3,8,128,512]{3,1,2,0:T(8,128)S(1)} fusion(f32[8,3,128,512]{3,0,2,1:T(8,128)S(1)} %fusion.4, f32[3,32,128,512]{3,2,1,0:T(8,128)} %get-tuple-element.12, f32[32,32]{1,0:T(8,128)S(1)} %fusion.192, s32[]{:T(128)S(6)} %select_n.307), kind=kOutput, calls=%fused_computation.80 | convolution fusion | flops 605552640 | bytes 37752836 | tf_op jit(solution)/shard_map/jbcd,ab->jacd/dot_general | solution.py:30
  1317.4 24.1 %all-to-all-done.2 = f32[3,8,128,512]{3,2,0,1:T(8,128)} async-done(((f32[3,8,128,512]{3,2,0,1:T(8,128)}), f32[3,8,128,512]{3,2,0,1:T(8,128)}, u32[]{:S(2)}, u32[]{:S(2)}) %all-to-all-start.2) | async-done | bytes 6291488 | tf_op jit(solution)/shard_map/all_to_all | solution.py:219
  1478.7 55.4 %gather_fusion = f32[4096,6]{0,1:T(8,128)S(1)} fusion(f32[6,132,4096]{2,0,1:T(8,128)} %pad_maximum_fusion.6, s32[4096]{0:T(1024)S(1)} %reshape.412), kind=kCustom, calls=%fused_computation | custom fusion | bytes 229376 | tf_op jit(solution)/shard_map/gather | solution.py:240
  1547.4 17.8 %copy.175 = f32[6,128,4096]{2,1,0:T(8,128)} copy(f32[6,128,4096]{2,0,1:T(8,128)} %copy-done.1) | data formatting | bytes 25165824
  (122 shorter events, 321.8 us)
Async XLA Ops:
  12.5 9.6 copy-start.6
  35.2 14.0 copy-start.5
  35.2 14.0 copy-start.2
  74.7 99.7 %all-to-all-start.1 = ((f32[512,8,512]{2,0,1:T(8,128)}), f32[512,8,512]{2,0,1:T(8,128)}, u32[]{:S(2)}, u32[]{:S(2)}) async-start(f32[512,8,512]{2,0,1:T(8,128)} %copy.137), calls=%async_computation.1 | async-start | bytes 16777216 | tf_op jit(solution)/shard_map/all_to_all | solution.py:175
  174.4 99.0 %all-to-all-start = ((f32[512,8,512]{2,0,1:T(8,128)}), f32[512,8,512]{2,0,1:T(8,128)}, u32[]{:S(2)}, u32[]{:S(2)}) async-start(f32[512,8,512]{2,0,1:T(8,128)} %copy.131), calls=%async_computation | async-start | bytes 16777216 | tf_op jit(solution)/shard_map/all_to_all | solution.py:174
  179.3 766.8 %all-reduce.3.cloned.1.call-start = ((), (), s32[]{:S(2)}) async-start(), calls=%async_computation.5 | async-start | bytes 33554432 | tf_op jit(solution)/shard_map/psum | solution.py:202
  315.3 18.1 %copy-start.7 = (f32[32,128,512]{2,0,1:T(8,128)S(1)}, f32[32,128,512]{2,0,1:T(8,128)}, u32[]{:S(2)}) copy-start(f32[32,128,512]{2,0,1:T(8,128)} %get-tuple-element.15) | copy-start | bytes 25165828
  315.3 30.5 %slice-start.2 = ((s8[8388608]{0:T(1024)(128)(4,1)}), s8[4194304]{0:T(1024)(128)(4,1)S(1)}, s32[]{:S(2)}) async-start(s8[8388608]{0:T(1024)(128)(4,1)} %bitcast.219), calls=%async_computation.8 | async-start | bytes 8388608
  333.4 12.4 slice-start.3
  967.1 63.2 %copy-start.3 = (f32[1,32,128,512]{3,2,1,0:T(8,128)}, f32[1,32,128,512]{3,2,1,0:T(8,128)S(1)}, u32[]{:S(2)}) copy-start(f32[1,32,128,512]{3,2,1,0:T(8,128)S(1)} %get-tuple-element.19) | copy-start | bytes 25165828
  967.1 63.2 %copy-start.4 = (f32[1,32,128,512]{3,2,1,0:T(8,128)}, f32[1,32,128,512]{3,2,1,0:T(8,128)S(1)}, u32[]{:S(2)}) copy-start(f32[1,32,128,512]{3,2,1,0:T(8,128)S(1)} %get-tuple-element.29) | copy-start | bytes 25165828
  1119.6 34.6 %copy-start = (f32[3,32,128,512]{3,2,1,0:T(8,128)S(1)}, f32[3,32,128,512]{3,2,1,0:T(8,128)}, u32[]{:S(2)}) copy-start(f32[3,32,128,512]{3,2,1,0:T(8,128)} %get-tuple-element.12) | copy-start | bytes 75497472
  1186.7 78.0 %all-to-all-start.3 = ((f32[3,8,128,512]{3,2,0,1:T(8,128)}), f32[3,8,128,512]{3,2,0,1:T(8,128)}, u32[]{:S(2)}, u32[]{:S(2)}) async-start(f32[3,8,128,512]{3,2,0,1:T(8,128)} %copy.158), calls=%async_computation.3 | async-start | bytes 12582912 | tf_op jit(solution)/shard_map/all_to_all | solution.py:220
  1264.7 6.0 copy-start.13
  1264.7 6.0 copy-start.14
  1264.8 76.7 %all-to-all-start.2 = ((f32[3,8,128,512]{3,2,0,1:T(8,128)}), f32[3,8,128,512]{3,2,0,1:T(8,128)}, u32[]{:S(2)}, u32[]{:S(2)}) async-start(f32[3,8,128,512]{3,2,0,1:T(8,128)} %copy.153), calls=%async_computation.2 | async-start | bytes 12582912 | tf_op jit(solution)/shard_map/all_to_all | solution.py:219
  1291.2 13.7 copy-start.8
  1357.4 13.9 copy-start.9
  1386.8 19.0 %slice-start = ((s8[6291456]{0:T(1024)(128)(4,1)}), s8[4194304]{0:T(1024)(128)(4,1)S(1)}, s32[]{:S(2)}) async-start(s8[6291456]{0:T(1024)(128)(4,1)} %bitcast.214), calls=%async_computation.6 | async-start | bytes 8388608
  1396.1 9.7 slice-start.1
  1462.6 9.6 copy-start.1
  1462.7 9.5 collective-permute-start
  1462.8 9.5 collective-permute-start.1
  1543.8 21.4 %all-to-all-start.4 = ((f32[8,1,384]{2,1,0:T(1,128)}), f32[8,1,384]{2,1,0:T(1,128)S(1)}, u32[]{:S(2)}, u32[]{:S(2)}) async-start(f32[8,1,384]{2,1,0:T(1,128)} %reshape.439), calls=%async_computation.4 | async-start | bytes 24576 | tf_op jit(solution)/shard_map/all_to_all | solution.py:256
  (3 other events, 17.0 us)
Sparse Core Ops, SparseCore 0:
  382.6 563.4 all-reduce.2
where the time goes:
time: 1590 us; the launch traced here: 1570 us
  waiting for transfers between devices  694 us (44%)
  matrix products  619 us (39%)
  local copies, waits for them, and re-layouts  172 us (11%)
  other arithmetic  44.5 us (3%)
  starting transfers between devices  29 us (2%)
  between operations  16.2 us (1%)
    dot_general x30, matrix products, product(): return jnp.einsum(formula, operand_a, operand_b, precision=HIGH)  618 us
    psum x1, waiting for transfers between devices, per_device(): summed = lax.psum((continued[0], continued[1]), 'depth')  563 us
    gather x2, local copies, waits for them, and re-layouts, per_device(): neighbours = padded[:, row_ids[:, :, None], col_ids[:, None, :]]  59.5 us
    all_to_all x1, waiting for transfers between devices, per_device(): lax.all_to_all(row_spectra[0], 'wide', split_axis=1, concat_axis=0, tiled...  57.7 us
    all_to_all x1, waiting for transfers between devices, per_device(): lax.all_to_all(row_spectra[1], 'wide', split_axis=1, concat_axis=0, tiled...  44.9 us
  transfers between devices with their start and end apart: 8, of which 5 were waited for; matrix products, arithmetic and copies ran while one was open for 14% of the time, Pallas kernels for 0%

commit v1 on v0

v1 whole, which is shorter than its diff:
```python
import functools
import math

import jax
import jax.numpy as jnp
import ml_dtypes
import numpy as np
from jax import lax
from jax.experimental import pallas as pl
from jax.experimental.pallas import tpu as pltpu
from jax.sharding import PartitionSpec as P

RADIX = 128
QLEV = 16
HALF = 64
SLOTS = 16
FIELDS = 5
HIGH = lax.Precision.HIGHEST
VMEM_LIMIT = 56 * 1024 * 1024


def np_split(table):
    high = table.astype(np.float32).astype(ml_dtypes.bfloat16)
    low = (table - high.astype(np.float64)).astype(ml_dtypes.bfloat16)
    return jnp.asarray(high), jnp.asarray(low)


def f32(table):
    return jnp.asarray(np.asarray(table, np.float32))


def angles(left, right, period):
    return (np.outer(left, right) % period) * (2.0 * math.pi / period)


def lane_order():
    column = np.arange(256)
    wave = (column // 128) * HALF + column % HALF
    return wave, (column % 128) // HALF


def slot_zero_angles(grid_len):
    wave, part = lane_order()
    outer_len = grid_len // RADIX
    upper = wave >= HALF
    freq = np.where(upper, outer_len // 2 + outer_len * (wave - HALF), outer_len * wave)
    return wave, part, upper, angles(np.arange(RADIX), freq, grid_len)


def row_forward_tables(grid_len):
    outer_len = grid_len // RADIX
    theta = angles(np.arange(SLOTS), np.arange(outer_len), outer_len)
    first = np.zeros((2 * SLOTS, outer_len))
    first[0::2] = np.cos(theta)
    first[1::2] = -np.sin(theta)
    first[1] = np.cos(np.pi * np.arange(outer_len))
    kron = np.kron(first, np.eye(8))
    wave, part = lane_order()
    alpha = angles(np.arange(RADIX), wave, RADIX)
    base = np.concatenate(
        [
            np.where(part == 0, np.cos(alpha), -np.sin(alpha)),
            np.where(part == 0, np.sin(alpha), np.cos(alpha)),
        ]
    )
    wave, part, upper, alpha = slot_zero_angles(grid_len)
    table = np.where(part == 0, np.cos(alpha), -np.sin(alpha))
    top = np.where(upper, 0.0, table)
    top[:, (wave == 0) & (part == 1)] = np.cos(np.pi * np.arange(RADIX))[:, None]
    zero = np.concatenate([top, np.where(upper, table, 0.0)])
    beta = 2.0 * math.pi * np.arange(RADIX)[:, None] / grid_len * np.ones((1, 256))
    return kron, base, zero, np.cos(beta), np.sin(beta)


def row_inverse_tables(grid_len):
    outer_len = grid_len // RADIX
    theta = angles(np.arange(outer_len), np.arange(SLOTS), outer_len)
    last = np.zeros((outer_len, 2 * SLOTS))
    last[:, 0::2] = np.cos(theta)
    last[:, 1::2] = -np.sin(theta)
    last[:, 1] = np.cos(np.pi * np.arange(outer_len))
    kron = np.kron(last, np.eye(8))
    wave, part = lane_order()
    alpha = angles(wave, np.arange(RADIX), RADIX)
    real_row = (part == 0)[:, None]
    base = 2.0 * np.concatenate(
        [
            np.where(real_row, np.cos(alpha), -np.sin(alpha)),
            np.where(real_row, np.sin(alpha), np.cos(alpha)),
        ],
        axis=1,
    )
    wave, part, upper, alpha = slot_zero_angles(grid_len)
    table = 2.0 * np.where(part == 0, np.cos(alpha), -np.sin(alpha))
    left = np.where(upper, 0.0, table)
    left[:, (wave == 0) & (part == 0)] = 1.0
    left[:, (wave == 0) & (part == 1)] = np.cos(np.pi * np.arange(RADIX))[:, None]
    zero = np.concatenate([left.T, np.where(upper, table, 0.0).T], axis=1)
    beta = 2.0 * math.pi * np.arange(RADIX)[None, :] / grid_len
    return kron, base, zero, np.cos(beta), np.sin(beta)


def column_kron(outer_len, orient):
    theta = angles(np.arange(outer_len), np.arange(outer_len), outer_len)
    return np.concatenate(
        [np.kron(np.cos(theta), np.eye(8)), np.kron(orient * np.sin(theta), np.eye(8))], axis=1
    )


def split(value):
    high = value.astype(jnp.bfloat16)
    return high, (value - high.astype(jnp.float32)).astype(jnp.bfloat16)


def mm(left, right):
    return jnp.dot(left, right, preferred_element_type=jnp.float32)


def dot3(left, right):
    return mm(left[0], right[0]) + mm(left[0], right[1]) + mm(left[1], right[0])


def rotate(value):
    lane = lax.broadcasted_iota(jnp.int32, value.shape, 1)
    return jnp.where(lane < HALF, -1.0, 1.0) * pltpu.roll(value, HALF, 1)


def row_forward_kernel(chunks, x_ref, kh, kl, base, zero, cw, sw, *refs):
    outs = refs[:chunks]
    th, tl, rot, u_ref = refs[chunks:]
    rows = x_ref.shape[0]
    outer_len = x_ref.shape[1] // RADIX

    @pl.when(pl.program_id(0) == 0)
    def _():
        th[0], tl[0] = split(zero[...])
        rot[...] = base[...]
        for slot in range(1, SLOTS):
            top, low = rot[0:RADIX, :], rot[RADIX:, :]
            rot[0:RADIX, :] = cw[...] * top - sw[...] * low
            rot[RADIX:, :] = cw[...] * low + sw[...] * top
            th[slot], tl[slot] = split(rot[...])

    table = (kh[...], kl[...])

    def first(pair, carry):
        halves = [
            jnp.concatenate(
                [
                    x_ref[pl.ds(pair * 16 + 8 * side, 8), RADIX * a : RADIX * (a + 1)]
                    for a in range(outer_len)
                ],
                axis=0,
            )
            for side in range(2)
        ]
        u_ref[pair] = dot3(table, split(jnp.concatenate(halves, axis=1)))
        return carry

    lax.fori_loop(0, rows // 16, first, 0)
    for slot in range(SLOTS):
        parts = []
        for part in range(2):
            at = 16 * slot + 8 * part
            parts.append(
                jnp.concatenate(
                    [
                        u_ref[pair, at : at + 8, RADIX * side : RADIX * (side + 1)]
                        for pair in range(rows // 16)
                        for side in range(2)
                    ],
                    axis=0,
                )
            )
        result = dot3(split(jnp.concatenate(parts, axis=1)), (th[slot], tl[slot]))
        for side in range(2):
            block = 2 * slot + side
            outs[block % chunks][block // chunks] = result[:, RADIX * side : RADIX * (side + 1)]


def full_spec(shape):
    return pl.BlockSpec(shape, lambda *_: (0,) * len(shape))


def row_forward(field, wide_count):
    rows, grid_len = field.shape
    chunks = 2 * SLOTS // wide_count
    step = min(rows, 128)
    kron, base, zero, cw, sw = row_forward_tables(grid_len)
    tables = (*np_split(kron), f32(base), f32(zero), f32(cw), f32(sw))
    return pl.pallas_call(
        functools.partial(row_forward_kernel, chunks),
        grid=(rows // step,),
        in_specs=[pl.BlockSpec((step, grid_len), lambda i: (i, 0))]
        + [full_spec(item.shape) for item in tables],
        out_specs=[pl.BlockSpec((wide_count, step, RADIX), lambda i: (0, i, 0))] * chunks,
        out_shape=[jax.ShapeDtypeStruct((wide_count, rows, RADIX), jnp.float32)] * chunks,
        scratch_shapes=[
            pltpu.VMEM((SLOTS, 256, 256), jnp.bfloat16),
            pltpu.VMEM((SLOTS, 256, 256), jnp.bfloat16),
            pltpu.VMEM((256, 256), jnp.float32),
            pltpu.VMEM((step // 16, 256, 256), jnp.float32),
        ],
        compiler_params=pltpu.CompilerParams(vmem_limit_bytes=VMEM_LIMIT),
        cost_estimate=pl.CostEstimate(
            flops=12 * rows * grid_len * 256, bytes_accessed=8 * rows * grid_len, transcendentals=0
        ),
        name="row_forward",
    )(field, *tables)


def wave_y(first, shape, grid_len):
    outer_len = grid_len // RADIX
    index = first + outer_len * lax.broadcasted_iota(jnp.int32, shape, 0)
    signed = jnp.where(index < grid_len // 2, index, index - grid_len).astype(jnp.float32)
    full = signed * (2.0 * math.pi / grid_len)
    return full, jnp.where(index == grid_len // 2, 0.0, full)


def column_forward_kernel(
    grid_len, depth_ref, x_ref, kx_ref, kh, kl, ca, sa, cw, sw, out_ref, u_ref, c_ref, s_ref
):
    outer_len = grid_len // RADIX
    table = (kh[...], kl[...])

    def first(pair, carry):
        halves = [
            jnp.concatenate(
                [x_ref[pl.ds(a * RADIX + pair * 16 + 8 * side, 8), :] for a in range(outer_len)],
                axis=0,
            )
            for side in range(2)
        ]
        turned = [rotate(half) for half in halves]
        data = jnp.concatenate(
            [jnp.concatenate(halves, axis=1), jnp.concatenate(turned, axis=1)], axis=0
        )
        result = dot3(table, split(data))
        for k1 in range(outer_len):
            for side in range(2):
                u_ref[pl.ds(k1 * RADIX + pair * 16 + 8 * side, 8), :] = result[
                    8 * k1 : 8 * k1 + 8, RADIX * side : RADIX * (side + 1)
                ]
        return carry

    lax.fori_loop(0, RADIX // 16, first, 0)
    c_ref[...] = ca[...]
    s_ref[...] = sa[...]
    top, thick = depth_ref[0], depth_ref[1]

    def second(k1, carry):
        cosine, sine = c_ref[...], s_ref[...]
        table = split(jnp.concatenate([cosine, sine], axis=1))
        c_ref[...] = cosine * cw[...] - sine * sw[...]
        s_ref[...] = sine * cw[...] + cosine * sw[...]
        rows = pl.ds(pl.multiple_of(k1 * RADIX, RADIX), RADIX)
        data = u_ref[rows, :]
        result = dot3(table, split(jnp.concatenate([data, rotate(data)], axis=0)))
        full_y, _ = wave_y(k1, (RADIX, RADIX), grid_len)
        magnitude = jnp.sqrt(kx_ref[...] * kx_ref[...] + full_y * full_y)
        scale = (1.0 - jnp.exp(-magnitude * thick)) * jnp.exp(-magnitude * top)
        out_ref[rows, :] = result * (scale * (2.0 * math.pi / (grid_len * grid_len)))
        return carry

    lax.fori_loop(0, outer_len, second, 0, unroll=2)


def column_forward(block, wave_x, depths):
    grid_len = block.shape[0]
    outer_len = grid_len // RADIX
    alpha = angles(np.arange(RADIX), np.arange(RADIX), RADIX)
    beta = 2.0 * math.pi * np.arange(RADIX)[None, :] / grid_len
    tables = (
        *np_split(column_kron(outer_len, -1.0)),
        f32(np.cos(alpha)),
        f32(-np.sin(alpha)),
        f32(np.cos(beta)),
        f32(-np.sin(beta)),
    )
    square = (RADIX, RADIX)
    return pl.pallas_call(
        functools.partial(column_forward_kernel, grid_len),
        in_specs=[pl.BlockSpec(memory_space=pltpu.SMEM)]
        + [pl.BlockSpec(memory_space=pltpu.VMEM)] * (2 + len(tables)),
        out_specs=pl.BlockSpec(memory_space=pltpu.VMEM),
        out_shape=jax.ShapeDtypeStruct(block.shape, jnp.float32),
        scratch_shapes=[
            pltpu.VMEM((grid_len, RADIX), jnp.float32),
            pltpu.VMEM(square, jnp.float32),
            pltpu.VMEM(square, jnp.float32),
        ],
        compiler_params=pltpu.CompilerParams(vmem_limit_bytes=VMEM_LIMIT),
        cost_estimate=pl.CostEstimate(
            flops=24 * grid_len * RADIX * 256,
            bytes_accessed=8 * grid_len * RADIX,
            transcendentals=2 * grid_len * RADIX,
        ),
        name="column_forward",
    )(depths, block, wave_x, *tables)


def column_inverse_kernel(
    grid_len, tile_rows, special, flag_ref, s_in, kx_ref, kxo_ref, bh, bl, ca, sa, cw, sw, *refs
):
    if special:
        edge_ref, out_ref, v_ref, c_ref, s_ref = refs
    else:
        out_ref, v_ref, c_ref, s_ref = refs
    outer_len = grid_len // RADIX
    here = bh.shape[0] // 8
    c_ref[...] = ca[...]
    s_ref[...] = sa[...]

    def first(k1, carry):
        cosine, sine = c_ref[...], s_ref[...]
        table = split(jnp.concatenate([cosine, sine], axis=1))
        c_ref[...] = cosine * cw[...] - sine * sw[...]
        s_ref[...] = sine * cw[...] + cosine * sw[...]
        rows = pl.ds(pl.multiple_of(k1 * RADIX, RADIX), RADIX)
        full_y, odd_y = wave_y(k1, (RADIX, RADIX), grid_len)
        full_x, odd_x = kx_ref[...], kxo_ref[...]
        squared = full_x * full_x + full_y * full_y
        safe = jnp.where(squared > 0.0, squared, 1.0)
        root = lax.rsqrt(safe)
        inverse = root * root
        value = s_in[rows, :]
        turned = rotate(value)
        coef_xx = -full_x * full_x * inverse
        coef_xy = -odd_x * odd_y * inverse
        coef_yy = -full_y * full_y * inverse
        slope_x = odd_x * root
        slope_y = odd_y * root
        upper = [
            value * coef_xx,
            value * coef_xy,
            turned * slope_x,
            value * coef_yy,
            turned * slope_y,
        ]
        lower = [
            turned * coef_xx,
            turned * coef_xy,
            -value * slope_x,
            turned * coef_yy,
            -value * slope_y,
        ]
        data = jnp.concatenate(
            [jnp.concatenate(upper, axis=1), jnp.concatenate(lower, axis=1)], axis=0
        )
        v_ref[rows, :] = dot3(table, split(data))
        return carry

    lax.fori_loop(0, outer_len, first, 0)
    both = jnp.concatenate([bh[...], bl[...]], axis=0)
    span = 8 * here

    def second(group, carry):
        data = jnp.concatenate(
            [v_ref[pl.ds(k1 * RADIX + group * 8, 8), :] for k1 in range(outer_len)], axis=0
        )
        turned = jnp.concatenate(
            [rotate(data[:, RADIX * c : RADIX * (c + 1)]) for c in range(FIELDS)], axis=1
        )
        high, low = split(jnp.concatenate([data, turned], axis=0))
        stacked = mm(both, high)
        result = stacked[:span] + stacked[span:] + mm(bh[...], low)
        per_row = RADIX // tile_rows
        row = (group * 8) % tile_rows
        for a in range(here):
            dest = a * per_row + (group * 8) // tile_rows
            for c in range(FIELDS):
                piece = result[8 * a : 8 * a + 8, RADIX * c : RADIX * (c + 1)]
                if special:
                    lane = lax.broadcasted_iota(jnp.int32, piece.shape, 1)
                    edge = edge_ref[c, pl.ds(a * RADIX + group * 8, 8), :]
                    edge = jnp.where(lane < HALF, edge[:, 0:1], edge[:, 1:2])
                    piece = jnp.where((lane % HALF == 0) & (flag_ref[0] == 0), edge, piece)
                out_ref[dest, c, pl.ds(row, 8), :] = piece
        return carry

    lax.fori_loop(0, RADIX // 8, second, 0)


def column_inverse(block, wave_x, odd_x, share, flag, edge, wide_count, tile_rows):
    grid_len = block.shape[0]
    alpha = angles(np.arange(RADIX), np.arange(RADIX), RADIX)
    beta = 2.0 * math.pi * np.arange(RADIX)[:, None] / grid_len * np.ones((1, RADIX))
    tables = (
        *share,
        f32(np.cos(alpha)),
        f32(np.sin(alpha)),
        f32(np.cos(beta)),
        f32(np.sin(beta)),
    )
    if edge is not None:
        tables = tables + (edge,)
    square = (RADIX, RADIX)
    out_shape = (wide_count, FIELDS, tile_rows, RADIX)
    return pl.pallas_call(
        functools.partial(column_inverse_kernel, grid_len, tile_rows, edge is not None),
        in_specs=[pl.BlockSpec(memory_space=pltpu.SMEM)]
        + [pl.BlockSpec(memory_space=pltpu.VMEM)] * (3 + len(tables)),
        out_specs=pl.BlockSpec(memory_space=pltpu.VMEM),
        out_shape=jax.ShapeDtypeStruct(out_shape, jnp.float32),
        scratch_shapes=[
            pltpu.VMEM((grid_len, FIELDS * RADIX), jnp.float32),
            pltpu.VMEM(square, jnp.float32),
            pltpu.VMEM(square, jnp.float32),
        ],
        compiler_params=pltpu.CompilerParams(vmem_limit_bytes=VMEM_LIMIT),
        cost_estimate=pl.CostEstimate(
            flops=FIELDS * 18 * grid_len * RADIX * 256,
            bytes_accessed=4 * (grid_len * RADIX + math.prod(out_shape)),
            transcendentals=grid_len * RADIX,
        ),
        name="column_inverse",
    )(flag, block, wave_x, odd_x, *tables)


def row_inverse_kernel(chunks, *refs):
    ins = refs[:chunks]
    kh, kl, base, zero, cw, sw, out_ref, th, tl, rot, u_ref = refs[chunks:]
    rows = ins[0].shape[2]
    outer_len = out_ref.shape[2] // RADIX

    @pl.when(pl.program_id(0) == 0)
    def _():
        th[0], tl[0] = split(zero[...])
        rot[...] = base[...]
        for slot in range(1, SLOTS):
            left, right = rot[:, 0:RADIX], rot[:, RADIX:]
            rot[:, 0:RADIX] = cw[...] * left - sw[...] * right
            rot[:, RADIX:] = cw[...] * right + sw[...] * left
            th[slot], tl[slot] = split(rot[...])

    for slot in range(SLOTS):
        parts = []
        for side in range(2):
            block = 2 * slot + side
            item = ins[block % chunks][block // chunks]
            parts.append(item.reshape(FIELDS * rows, RADIX))
        u_ref[slot] = dot3(split(jnp.concatenate(parts, axis=1)), (th[slot], tl[slot]))

    table = (kh[...], kl[...])
    for c in range(FIELDS):

        def second(pair, carry):
            halves = []
            for side in range(2):
                at = pl.ds(c * rows + pair * 16 + 8 * side, 8)
                halves.append(
                    jnp.concatenate(
                        [
                            u_ref[slot, at, RADIX * part : RADIX * (part + 1)]
                            for slot in range(SLOTS)
                            for part in range(2)
                        ],
                        axis=0,
                    )
                )
            result = dot3(table, split(jnp.concatenate(halves, axis=1)))
            for a in range(outer_len):
                for side in range(2):
                    out_ref[
                        c, pl.ds(pair * 16 + 8 * side, 8), RADIX * a : RADIX * (a + 1)
                    ] = result[8 * a : 8 * a + 8, RADIX * side : RADIX * (side + 1)]
            return carry

        lax.fori_loop(0, rows // 16, second, 0)
    out_ref[FIELDS] = -(out_ref[0] + out_ref[3])


def row_inverse(blocks, grid_len):
    chunks = len(blocks)
    wide_count, _, rows, _ = blocks[0].shape
    step = min(rows, 32)
    kron, base, zero, cw, sw = row_inverse_tables(grid_len)
    tables = (*np_split(kron), f32(base), f32(zero), f32(cw), f32(sw))
    return pl.pallas_call(
        functools.partial(row_inverse_kernel, chunks),
        grid=(rows // step,),
        in_specs=[pl.BlockSpec((wide_count, FIELDS, step, RADIX), lambda i: (0, 0, i, 0))] * chunks
        + [full_spec(item.shape) for item in tables],
        out_specs=pl.BlockSpec((FIELDS + 1, step, grid_len), lambda i: (0, i, 0)),
        out_shape=jax.ShapeDtypeStruct((FIELDS + 1, rows, grid_len), jnp.float32),
        scratch_shapes=[
            pltpu.VMEM((SLOTS, 256, 256), jnp.bfloat16),
            pltpu.VMEM((SLOTS, 256, 256), jnp.bfloat16),
            pltpu.VMEM((256, 256), jnp.float32),
            pltpu.VMEM((SLOTS, FIELDS * step, 256), jnp.float32),
        ],
        compiler_params=pltpu.CompilerParams(vmem_limit_bytes=VMEM_LIMIT),
        cost_estimate=pl.CostEstimate(
            flops=12 * FIELDS * rows * grid_len * 256,
            bytes_accessed=44 * rows * grid_len,
            transcendentals=0,
        ),
        name="row_inverse",
    )(*blocks, *tables)


def interpolate_kernel(g_ref, halo_ref, wy_ref, col_ref, wx_ref, place_ref, out_ref, mask_ref):
    samples, grid_len = mask_ref.shape
    wide = 512

    @pl.when(pl.program_id(0) == 0)
    def _():
        for start in range(0, grid_len, wide):
            lane = start + lax.broadcasted_iota(jnp.int32, (samples, wide), 1)
            total = jnp.zeros((samples, wide), jnp.float32)
            for tap in range(4):
                total = total + jnp.where(
                    lane == col_ref[:, tap : tap + 1], wx_ref[:, tap : tap + 1], 0.0
                )
            mask_ref[:, start : start + wide] = total

    left = split(wy_ref[...])
    partial = jnp.zeros((samples, RADIX), jnp.float32)
    for start in range(0, grid_len, wide):
        at = slice(start, start + wide)
        data = jnp.concatenate([g_ref[0, :, at], halo_ref[0, :, at]], axis=0)
        product = dot3(left, split(data)) * mask_ref[:, at]
        for lane in range(0, wide, RADIX):
            partial = partial + product[:, lane : lane + RADIX]
    value = jnp.sum(partial, axis=1, keepdims=True)
    out_ref[0] = jnp.sum(value * place_ref[...], axis=0, keepdims=True)


def interpolate(gradient, halo, weight_y, col_ids, weight_x, placement):
    fields, rows, grid_len = gradient.shape
    samples, slot_total = placement.shape
    small = (weight_y, col_ids, weight_x, placement)
    return pl.pallas_call(
        interpolate_kernel,
        grid=(fields,),
        in_specs=[
            pl.BlockSpec((1, rows, grid_len), lambda i: (i, 0, 0)),
            pl.BlockSpec((1, 8, grid_len), lambda i: (i, 0, 0)),
        ]
        + [full_spec(item.shape) for item in small],
        out_specs=pl.BlockSpec((1, 1, slot_total), lambda i: (i, 0, 0)),
        out_shape=jax.ShapeDtypeStruct((fields, 1, slot_total), jnp.float32),
        scratch_shapes=[pltpu.VMEM((samples, grid_len), jnp.float32)],
        compiler_params=pltpu.CompilerParams(vmem_limit_bytes=VMEM_LIMIT),
        name="interpolate",
    )(gradient, halo, *small)


def product(formula, operand_a, operand_b):
    return jnp.einsum(formula, operand_a, operand_b, precision=HIGH)


def complex_product(formula, pair, table):
    return (
        product(formula, pair[0], table[0]) - product(formula, pair[1], table[1]),
        product(formula, pair[0], table[1]) + product(formula, pair[1], table[0]),
    )


def phase(row_count, col_count, period, orient):
    theta = angles(np.arange(row_count), np.arange(col_count), period)
    return f32(np.cos(theta)), f32(orient * np.sin(theta))


def times_table(pair, table):
    return (
        pair[0] * table[0] - pair[1] * table[1],
        pair[0] * table[1] + pair[1] * table[0],
    )


def edge_waves(grid_len):
    outer_len = grid_len // RADIX
    index = np.arange(outer_len)[:, None] + outer_len * np.arange(RADIX)[None, :]
    signed = np.where(index < grid_len // 2, index, index - grid_len).astype(np.float32)
    full_y = signed * np.float32(2.0 * math.pi / grid_len)
    odd_y = np.where(index == grid_len // 2, np.float32(0.0), full_y)
    return full_y, odd_y


def edge_forward(values, layer_top, layer_thick):
    grid_len = values.shape[1]
    outer_len = grid_len // RADIX
    columns = values.reshape(2, outer_len, RADIX)
    first = phase(outer_len, outer_len, outer_len, -1.0)
    pair = (product("zab,ka->zkb", columns, first[0]), product("zab,ka->zkb", columns, first[1]))
    pair = times_table(pair, phase(outer_len, RADIX, grid_len, -1.0))
    pair = complex_product("zkb,bc->zkc", pair, phase(RADIX, RADIX, RADIX, -1.0))
    full_y, _ = edge_waves(grid_len)
    magnitude = jnp.sqrt(
        jnp.asarray(np.stack([full_y * full_y, full_y * full_y + np.float32(math.pi) ** 2]))
    )
    scale = (
        2.0
        * math.pi
        / (grid_len * grid_len)
        * (1.0 - jnp.exp(-magnitude * layer_thick))
        * jnp.exp(-magnitude * layer_top)
    )
    return jnp.stack([pair[0] * scale, pair[1] * scale])


def edge_inverse(total, row_start, row_share):
    outer_len = total.shape[2]
    grid_len = outer_len * RADIX
    full_y, odd_y = edge_waves(grid_len)
    full_x = np.array([0.0, math.pi], np.float32)[:, None, None]
    squared = full_x * full_x + full_y * full_y
    safe = np.where(squared > 0.0, squared, np.float32(1.0))
    none = np.zeros_like(safe)
    plain = f32(np.stack([-full_x * full_x / safe, none, none, -full_y * full_y / safe, none]))
    turned = f32(np.stack([none, none, none, none, odd_y / np.sqrt(safe)]))
    pair = (total[0] * plain - total[1] * turned, total[1] * plain + total[0] * turned)
    pair = complex_product("fzkc,cb->fzkb", pair, phase(RADIX, RADIX, RADIX, 1.0))
    pair = times_table(pair, phase(outer_len, RADIX, grid_len, 1.0))
    last = phase(outer_len, outer_len, outer_len, 1.0)
    last = [lax.dynamic_slice_in_dim(item, row_start, row_share, 0) for item in last]
    real = product("fzkb,ak->fzab", pair[0], last[0]) - product("fzkb,ak->fzab", pair[1], last[1])
    return jnp.moveaxis(real.reshape(FIELDS, 2, row_share * RADIX), 1, 2)


def cubic_kernel(distance):
    near_part = (1.5 * distance - 2.5) * distance * distance + 1.0
    far_part = ((-0.5 * distance + 2.5) * distance - 4.0) * distance + 2.0
    return jnp.where(distance <= 1.0, near_part, jnp.where(distance < 2.0, far_part, 0.0))


def tap_weights(level):
    offset = (level.astype(jnp.float32) + 0.5) / QLEV - 0.5
    base = jnp.where(level < QLEV // 2, -1, 0).astype(jnp.int32)
    fraction = offset - base.astype(jnp.float32)
    taps = jnp.arange(4, dtype=jnp.int32)[None, :]
    weights = cubic_kernel(jnp.abs(fraction[:, None] - (taps.astype(jnp.float32) - 1.0)))
    return weights, base[:, None] - 1 + taps


def depth_sum(blocks):
    return [lax.psum(block, "depth") for block in blocks]


def per_device(density, layer_top, layer_thick, sample_row, sample_col, sample_frac, sample_owner):
    wide_count = lax.axis_size("wide")
    depth_count = lax.axis_size("depth")
    rows_here, grid_len = density.shape[1], density.shape[2]
    outer_len = grid_len // RADIX
    tile_rows = rows_here // depth_count
    chunks = 2 * SLOTS // wide_count
    wide_id, depth_id = lax.axis_index("wide"), lax.axis_index("depth")

    def exchange(block):
        return lax.all_to_all(block, "wide", split_axis=0, concat_axis=0, tiled=True)

    spectra = [exchange(item) for item in row_forward(density[0], wide_count)]
    columns = [item.reshape(grid_len, RADIX) for item in spectra]

    lane = jnp.arange(RADIX, dtype=jnp.int32)[None, :] % HALF
    waves = []
    for chunk in range(chunks):
        block = wide_id * chunks + chunk
        slot = block // 2
        place = (block % 2) * HALF + lane
        low = jnp.where(
            place < HALF, outer_len * place, outer_len // 2 + outer_len * (place - HALF)
        )
        index = jnp.where(slot == 0, low, slot + outer_len * place)
        signed = jnp.where(index < grid_len // 2, index, index - grid_len).astype(jnp.float32)
        waves.append(signed * (2.0 * math.pi / grid_len))

    depths = jnp.concatenate([layer_top, layer_thick])
    edge = edge_forward(
        jnp.stack([columns[0][:, 0], columns[0][:, HALF]]), layer_top[0], layer_thick[0]
    )
    summed = depth_sum([column_forward(c, w, depths) for c, w in zip(columns, waves)])
    row_share = outer_len // depth_count
    row_start = depth_id * row_share
    edge = edge_inverse(lax.psum(edge, "depth"), row_start, row_share)
    back = np_split(column_kron(outer_len, 1.0))
    share = [lax.dynamic_slice_in_dim(item, row_start * 8, row_share * 8, 0) for item in back]
    flag = wide_id.astype(jnp.int32).reshape(1)
    blocks = []
    for chunk in range(chunks):
        item = column_inverse(
            summed[chunk],
            waves[chunk],
            waves[chunk],
            share,
            flag,
            edge if chunk == 0 else None,
            wide_count,
            tile_rows,
        )
        blocks.append(exchange(item))
    gradient = row_inverse(blocks, grid_len)

    tiles = depth_count * wide_count
    forward = [(i, (i + 1) % tiles) for i in range(tiles)]
    backward = [(target, source) for source, target in forward]
    low = lax.ppermute(gradient[:, tile_rows - 2 :], ("depth", "wide"), forward)
    high = lax.ppermute(gradient[:, :2], ("depth", "wide"), backward)
    halo = jnp.concatenate(
        [low, high, jnp.zeros((FIELDS + 1, 4, grid_len), jnp.float32)], axis=1
    )

    taps_y, offset_y = tap_weights(sample_frac[0, 0])
    taps_x, offset_x = tap_weights(sample_frac[0, 1])
    row_ids = sample_row[0][:, None] + offset_y
    col_ids = (sample_col[0][:, None] + offset_x) % grid_len
    row_ids = jnp.where(
        row_ids < 0,
        row_ids + tile_rows + 2,
        jnp.where(row_ids >= tile_rows, row_ids + 2, row_ids),
    )
    row_marks = row_ids[:, :, None] == jnp.arange(tile_rows + 8, dtype=jnp.int32)
    weight_y = jnp.sum(jnp.where(row_marks, taps_y[:, :, None], 0.0), axis=1)
    sample_count = sample_row.shape[1]
    capacity = max(2 * sample_count // wide_count, 2)
    slot_total = wide_count * capacity
    owner_ids = sample_owner[0, :, 0]
    same = owner_ids[:, None] == owner_ids[None, :]
    order = jnp.arange(sample_count, dtype=jnp.int32)
    slot_ids = jnp.sum((same & (order[None, :] < order[:, None])).astype(jnp.int32), axis=1)
    target = owner_ids * capacity + slot_ids
    placement = (target[:, None] == jnp.arange(slot_total, dtype=jnp.int32)[None, :]).astype(
        jnp.float32
    )
    outgoing = interpolate(gradient, halo, weight_y, col_ids, taps_x, placement)
    outgoing = outgoing.reshape(FIELDS + 1, wide_count, capacity)
    arrived = lax.all_to_all(outgoing, "wide", split_axis=1, concat_axis=1, tiled=True)
    return (gradient, arrived.reshape(FIELDS + 1, 1, slot_total))


def solution(mesh):
    in_specs = (
        P("depth", "wide", None),
        P("depth"),
        P("depth"),
        P(("depth", "wide"), None),
        P(("depth", "wide"), None),
        P(("depth", "wide"), None, None),
        P(("depth", "wide"), None, None),
    )
    out_specs = (P(None, ("depth", "wide"), None), P(None, ("depth", "wide"), None))
    return jax.shard_map(
        per_device, mesh=mesh, in_specs=in_specs, out_specs=out_specs, check_vma=False
    )
```

time: 1590 us -> 720 us (0.45)
  matrix products: 619 us -> 4.02 us
  waiting for transfers between devices: 694 us -> 371 us
  Pallas kernels: 0 us -> 209 us
  local copies, waits for them, and re-layouts: 172 us -> 13.5 us
  blocking collectives: 0 us -> 68.9 us
  other arithmetic: 44.5 us -> 7.83 us
    dot_general x30 -> x12, matrix products: 618 us -> 4.02 us  [product(): return jnp.einsum(formula, operand_a, operand_b, precision=HIGH)]
    psum x1, waiting for transfers between devices: 563 us -> 296 us  [depth_sum(): return [lax.psum(block, 'depth') for block in blocks]]
    pallas_call x0 -> x11, Pallas kernels: none -> 209 us  [the longest x4 104 us: column_inverse(): pl.pallas_call(functools.partial(column_inverse_kernel, grid_len, tile_ro...]
    all_to_all x0 -> x3, blocking collectives: none -> 68.9 us  [the longest x2 61.8 us: exchange(): lax.all_to_all(block, 'wide', split_axis=0, concat_axis=0, tiled=True)]
    gather x2 -> x0, local copies, waits for them, and re-layouts: 59.5 us -> none  [per_device(): neighbours = padded[:, row_ids[:, :, None], col_ids[:, None, :]]]
    all_to_all x5 -> x6, waiting for transfers between devices: 127 us -> 71.7 us  [exchange(): lax.all_to_all(block, 'wide', split_axis=0, concat_axis=0, tiled=True)]
    reshape x9 -> x3, local copies, waits for them, and re-layouts: 48.1 us -> 0.77 us  [the longest x1 0.68 us: per_device(): return (gradient, arrived.reshape(FIELDS + 1, 1, slot_total))]
    unnamed x43 -> x42, local copies, waits for them, and re-layouts: 26.3 us -> 3.28 us
  transfers between devices with their start and end apart: 8 -> 9, of which waited for: 5 -> 7; matrix products, arithmetic and copies ran while one was open for 14% -> 1% of each run, Pallas kernels for 0% -> 16%
where the time goes in v1:
time: 720 us; the launch traced here: 719 us
  waiting for transfers between devices  371 us (52%)
  Pallas kernels  209 us (29%)
  blocking collectives  68.9 us (10%)
  starting transfers between devices  29.7 us (4%)
  between operations  15.8 us (2%)
  local copies, waits for them, and re-layouts  13.5 us (2%)
  other arithmetic  7.83 us (1%)
    psum x1, waiting for transfers between devices, depth_sum(): return [lax.psum(block, 'depth') for block in blocks]  296 us
    pallas_call x4, Pallas kernels, column_inverse(): pl.pallas_call(functools.partial(column_inverse_kernel, grid_len, tile_ro...  104 us
    all_to_all x6, waiting for transfers between devices, exchange(): lax.all_to_all(block, 'wide', split_axis=0, concat_axis=0, tiled=True)  71.7 us
    all_to_all x2, blocking collectives, exchange(): lax.all_to_all(block, 'wide', split_axis=0, concat_axis=0, tiled=True)  61.8 us
    pallas_call x4, Pallas kernels, column_forward(): pl.pallas_call(functools.partial(column_forward_kernel, grid_len), in_spe...  49.7 us
    all_to_all x6, starting transfers between devices, exchange(): lax.all_to_all(block, 'wide', split_axis=0, concat_axis=0, tiled=True)  24.3 us
    pallas_call x1, Pallas kernels, row_inverse(): pl.pallas_call(functools.partial(row_inverse_kernel, chunks), grid=(rows...  20.6 us
    pallas_call x1, Pallas kernels, row_forward(): pl.pallas_call(functools.partial(row_forward_kernel, chunks), grid=(rows...  17.1 us
  transfers between devices with their start and end apart: 9, of which 7 were waited for; matrix products, arithmetic and copies ran while one was open for 1% of the time, Pallas kernels for 16%

profile of v1, /device:TPU:0, one launch (start us, length us, event | category | flops | bytes accessed | tf_op | source)
XLA Modules:
  0.0 718.9 jit_solution(5621212700440175349)
XLA Ops:
  7.2 17.1 %row_forward.1 = (f32[8,512,128]{2,1,0:T(8,128)}, f32[8,512,128]{2,1,0:T(8,128)}, f32[8,512,128]{2,1,0:T(8,128)}, f32[8,512,128]{2,1,0:T(8,128)}) custom-call(f32[512,4096]{1,0:T(8,128)} %bitcast.91, bf16[256,256]{1,0:T(8,128)(2,1)} %constant.234.clone.kh, bf16[256,256]{1,0:T(8,128)(2,1)} %constant.235.clone.kl, f32[256,256]{1,0:T(8,128)} %constant.236.clone.base, ...), custom_call_target="tpu_custom_call" | custom-call | flops 6442450944 | bytes 16777216 | tf_op jit(solution)/shard_map/row_forward/pallas_call | solution.py:191
  24.3 32.0 %all_to_all.45 = f32[8,512,128]{2,1,0:T(8,128)} all-to-all(f32[8,512,128]{2,1,0:T(8,128)} %get-tuple-element.8), channel_id=1, replica_groups=mesh['depth'=4,'wide'=8] {'wide'}, dimensions={0} | all-to-all | bytes 4194304 | tf_op jit(solution)/shard_map/all_to_all | solution.py:651
  56.3 29.8 %all_to_all.46 = f32[8,512,128]{2,1,0:T(8,128)} all-to-all(f32[8,512,128]{2,1,0:T(8,128)S(1)} %copy-done.5), channel_id=1, replica_groups=mesh['depth'=4,'wide'=8] {'wide'}, dimensions={0} | all-to-all | bytes 4194304 | tf_op jit(solution)/shard_map/all_to_all | solution.py:651
  92.8 23.5 %all-to-all-done = f32[8,512,128]{2,1,0:T(8,128)S(1)} async-done(((f32[8,512,128]{2,1,0:T(8,128)}), f32[8,512,128]{2,1,0:T(8,128)S(1)}, u32[]{:S(2)}, u32[]{:S(2)}) %all-to-all-start) | async-done | bytes 2097184 | tf_op jit(solution)/shard_map/all_to_all | solution.py:651
  116.2 4.4 all-to-all-start.2
  123.2 12.5 %column_forward.4 = f32[4096,128]{1,0:T(8,128)} custom-call(f32[2]{0:T(128)} %pad_maximum_fusion.4.depth_ref, f32[4096,128]{1,0:T(8,128)} %bitcast.73, f32[1,128]{1,0:T(1,128)} %get-tuple-element.36.kx_ref.kxo_ref, bf16[256,512]{1,0:T(8,128)(2,1)} %constant.247.clone.kh, bf16[256,512]{1,0:T(8,128)(2,1)} %constant.248.clone.kl, ...), custom_call_target="tpu_custom_call" | custom-call | flops 3221225472 | bytes 4194304 | tf_op jit(solution)/shard_map/column_forward/pallas_call | solution.py:281
  135.7 12.5 %column_forward.6 = f32[4096,128]{1,0:T(8,128)} custom-call(f32[2]{0:T(128)} %pad_maximum_fusion.4.depth_ref, f32[4096,128]{1,0:T(8,128)} %bitcast.76, f32[1,128]{1,0:T(1,128)} %get-tuple-element.34.kx_ref.kxo_ref, bf16[256,512]{1,0:T(8,128)(2,1)} %constant.247.clone.kh, bf16[256,512]{1,0:T(8,128)(2,1)} %constant.248.clone.kl, ...), custom_call_target="tpu_custom_call" | custom-call | flops 3221225472 | bytes 4194304 | tf_op jit(solution)/shard_map/column_forward/pallas_call | solution.py:281
  148.1 12.4 %column_forward.7 = f32[4096,128]{1,0:T(8,128)} custom-call(f32[2]{0:T(128)} %pad_maximum_fusion.4.depth_ref, f32[4096,128]{1,0:T(8,128)} %bitcast.75, f32[1,128]{1,0:T(1,128)} %get-tuple-element.33.kx_ref.kxo_ref, bf16[256,512]{1,0:T(8,128)(2,1)} %constant.247.clone.kh, bf16[256,512]{1,0:T(8,128)(2,1)} %constant.248.clone.kl, ...), custom_call_target="tpu_custom_call" | custom-call | flops 3221225472 | bytes 4194304 | tf_op jit(solution)/shard_map/column_forward/pallas_call | solution.py:281
  160.6 12.4 %column_forward.5 = f32[4096,128]{1,0:T(8,128)} custom-call(f32[2]{0:T(128)} %pad_maximum_fusion.4.depth_ref, f32[4096,128]{1,0:T(8,128)} %bitcast.28.x_ref, f32[1,128]{1,0:T(1,128)} %get-tuple-element.35.kx_ref.kxo_ref, bf16[256,512]{1,0:T(8,128)(2,1)} %constant.247.clone.kh, bf16[256,512]{1,0:T(8,128)(2,1)} %constant.248.clone.kl, ...), custom_call_target="tpu_custom_call" | custom-call | flops 3221225472 | bytes 4194304 | tf_op jit(solution)/shard_map/column_forward/pallas_call | solution.py:281
  175.6 296.3 %all-reduce.3.cloned.1.call-done = (f32[4096,128]{1,0:T(8,128)}, f32[2,2,32,128]{3,2,1,0:T(8,128)}, f32[4096,128]{1,0:T(8,128)}, f32[4096,128]{1,0:T(8,128)}, f32[4096,128]{1,0:T(8,128)}) async-done(((f32[4096,128]{1,0:T(8,128)}, f32[2,2,32,128]{3,2,1,0:T(8,128)}, f32[4096,128]{1,0:T(8,128)}, f32[4096,128]{1,0:T(8,128)}, f32[4096,128]{1,0:T(8,128)}), (f32[4096,128]{1,0:T(8,128)}, ...) | async-done | bytes 8454160 | tf_op jit(solution)/shard_map/psum | solution.py:638
  478.0 26.9 %column_inverse.4 = f32[8,5,128,128]{3,2,1,0:T(8,128)} custom-call(s32[1]{0:T(128)} %bitcast.flag_ref, f32[4096,128]{1,0:T(8,128)} %get-tuple-element.18.s_in, f32[1,128]{1,0:T(1,128)} %get-tuple-element.36.kx_ref.kxo_ref, f32[1,128]{1,0:T(1,128)} %get-tuple-element.36.kx_ref.kxo_ref, bf16[64,512]{1,0:T(8,128)(2,1)} %get-tuple-element.38.bh, ...), custom_call_target="tpu_custom_call" | custom-call | flops 12079595520 | bytes 4718592 | tf_op jit(solution)/shard_map/column_inverse/pallas_call | solution.py:399
  508.6 25.8 %column_inverse.6 = f32[8,5,128,128]{3,2,1,0:T(8,128)} custom-call(s32[1]{0:T(128)} %bitcast.flag_ref, f32[4096,128]{1,0:T(8,128)} %get-tuple-element.21.s_in, f32[1,128]{1,0:T(1,128)} %get-tuple-element.34.kx_ref.kxo_ref, f32[1,128]{1,0:T(1,128)} %get-tuple-element.34.kx_ref.kxo_ref, bf16[64,512]{1,0:T(8,128)(2,1)} %get-tuple-element.38.bh, ...), custom_call_target="tpu_custom_call" | custom-call | flops 12079595520 | bytes 4718592 | tf_op jit(solution)/shard_map/column_inverse/pallas_call | solution.py:399
  534.4 6.5 all-to-all-done.1.refs_0_
  542.4 4.6 all-to-all-start.5
  547.1 25.8 %column_inverse.7 = f32[8,5,128,128]{3,2,1,0:T(8,128)} custom-call(s32[1]{0:T(128)} %bitcast.flag_ref, f32[4096,128]{1,0:T(8,128)} %get-tuple-element.22.s_in, f32[1,128]{1,0:T(1,128)} %get-tuple-element.33.kx_ref.kxo_ref, f32[1,128]{1,0:T(1,128)} %get-tuple-element.33.kx_ref.kxo_ref, bf16[64,512]{1,0:T(8,128)(2,1)} %get-tuple-element.38.bh, ...), custom_call_target="tpu_custom_call" | custom-call | flops 12079595520 | bytes 4718592 | tf_op jit(solution)/shard_map/column_inverse/pallas_call | solution.py:399
  572.8 6.3 all-to-all-done.5.refs_2_
  582.8 25.8 %column_inverse.5 = f32[8,5,128,128]{3,2,1,0:T(8,128)} custom-call(s32[1]{0:T(128)} %bitcast.flag_ref, f32[4096,128]{1,0:T(8,128)} %get-tuple-element.20.s_in, f32[1,128]{1,0:T(1,128)} %get-tuple-element.35.kx_ref.kxo_ref, f32[1,128]{1,0:T(1,128)} %get-tuple-element.35.kx_ref.kxo_ref, bf16[64,512]{1,0:T(8,128)(2,1)} %get-tuple-element.38.bh, ...), custom_call_target="tpu_custom_call" | custom-call | flops 12079595520 | bytes 4718592 | tf_op jit(solution)/shard_map/column_inverse/pallas_call | solution.py:399
  608.6 6.4 all-to-all-done.7.refs_3_
  616.5 4.4 all-to-all-start.3
  624.2 29.0 %all-to-all-done.3.refs_1_ = f32[8,5,128,128]{3,2,1,0:T(8,128)} async-done(((f32[8,5,128,128]{3,2,1,0:T(8,128)}), f32[8,5,128,128]{3,2,1,0:T(8,128)}, u32[]{:S(2)}, u32[]{:S(2)}) %all-to-all-start.3) | async-done | bytes 2621472 | tf_op jit(solution)/shard_map/all_to_all | solution.py:651
  653.2 20.6 %row_inverse.1.g_ref = f32[6,128,4096]{2,1,0:T(8,128)} custom-call(f32[8,5,128,128]{3,2,1,0:T(8,128)} %copy-done.1, f32[8,5,128,128]{3,2,1,0:T(8,128)} %all-to-all-done.3.refs_1_, f32[8,5,128,128]{3,2,1,0:T(8,128)} %all-to-all-done.5.refs_2_, f32[8,5,128,128]{3,2,1,0:T(8,128)} %copy-done.2, bf16[256,256]{1,0:T(8,128)(2,1)} %constant.260.clone.refs_4_, ...), custom_call_target="tpu_custom_call" | custom-call | flops 8053063680 | bytes 23068672 | tf_op jit(solution)/shard_map/row_inverse/pallas_call | solution.py:479
  675.4 5.3 collective-permute-start.1
  685.2 16.9 %interpolate.1 = f32[6,1,512]{2,1,0:T(1,128)} custom-call(f32[6,128,4096]{2,1,0:T(8,128)} %row_inverse.1.g_ref, f32[6,8,4096]{2,1,0:T(8,128)} %maximum_maximum_fusion.halo_ref, f32[256,136]{1,0:T(8,128)} %copy.98.wy_ref, s32[256,4]{1,0:T(8,128)} %add_select_fusion.col_ref, f32[256,4]{1,0:T(8,128)} %get-tuple-element.31.wx_ref, f32[256,512]{1,0:T(8,128)} %fusion.5.place_ref), custom_call_target="tpu_custom_call" | custom-call | tf_op jit(solution)/shard_map/interpolate/pallas_call | solution.py:533
  703.0 7.1 all_to_all.47
  (95 shorter events, 39.0 us)
Async XLA Ops:
  24.3 32.0 %copy-start.5 = (f32[8,512,128]{2,1,0:T(8,128)S(1)}, f32[8,512,128]{2,1,0:T(8,128)}, u32[]{:S(2)}) copy-start(f32[8,512,128]{2,1,0:T(8,128)} %get-tuple-element.9) | copy-start | bytes 6291460
  86.0 30.2 %all-to-all-start = ((f32[8,512,128]{2,1,0:T(8,128)}), f32[8,512,128]{2,1,0:T(8,128)S(1)}, u32[]{:S(2)}, u32[]{:S(2)}) async-start(f32[8,512,128]{2,1,0:T(8,128)} %get-tuple-element.6), calls=%async_computation | async-start | bytes 4194304 | tf_op jit(solution)/shard_map/all_to_all | solution.py:651
  116.2 4.4 copy-start
  116.2 44.3 %all-to-all-start.2 = ((f32[8,512,128]{2,1,0:T(8,128)}), f32[8,512,128]{2,1,0:T(8,128)}, u32[]{:S(2)}, u32[]{:S(2)}) async-start(f32[8,512,128]{2,1,0:T(8,128)} %get-tuple-element.7), calls=%async_computation.2 | async-start | bytes 4194304 | tf_op jit(solution)/shard_map/all_to_all | solution.py:651
  120.6 351.4 %all-reduce.3.cloned.1.call-start = ((), (), s32[]{:S(2)}) async-start(), calls=%async_computation.9 | async-start | bytes 16908288 | tf_op jit(solution)/shard_map/psum | solution.py:638
  120.7 2.1 copy-start.6
  120.7 2.1 copy-start.9
  120.7 2.3 copy-start.11
  160.6 12.4 %copy-start.12 = (f32[2,32,128]{2,1,0:T(8,128)S(1)}, f32[2,32,128]{2,1,0:T(8,128)}, u32[]{:S(2)}) copy-start(f32[2,32,128]{2,1,0:T(8,128)} %constant.273) | copy-start | bytes 98308
  174.0 298.8 %copy-start.3 = (f32[5,2,32,128]{3,2,1,0:T(8,128)S(1)}, f32[5,2,32,128]{3,2,1,0:T(8,128)}, u32[]{:S(2)}) copy-start(f32[5,2,32,128]{3,2,1,0:T(8,128)} %constant.251.clone) | copy-start | bytes 491524
  174.0 298.8 %copy-start.4 = (f32[5,2,32,128]{3,2,1,0:T(8,128)S(1)}, f32[5,2,32,128]{3,2,1,0:T(8,128)}, u32[]{:S(2)}) copy-start(f32[5,2,32,128]{3,2,1,0:T(8,128)} %constant.252.clone) | copy-start | bytes 491524
  174.0 298.8 %copy-start.7 = (f32[128,128,1,1]{1,0,3,2:T(8,128)S(1)}, f32[128,128,1,1]{1,0,3,2:T(8,128)}, u32[]{:S(2)}) copy-start(f32[128,128,1,1]{1,0,3,2:T(8,128)} %constant.278) | copy-start | bytes 196612
  174.0 299.1 %copy-start.8 = (f32[128,128,1,1]{1,0,3,2:T(8,128)S(1)}, f32[128,128,1,1]{1,0,3,2:T(8,128)}, u32[]{:S(2)}) copy-start(f32[128,128,1,1]{1,0,3,2:T(8,128)} %constant.279) | copy-start | bytes 196612
  174.0 299.9 %copy-start.13 = (f32[32,128]{1,0:T(8,128)S(1)}, f32[32,128]{1,0:T(8,128)}, u32[]{:S(2)}) copy-start(f32[32,128]{1,0:T(8,128)} %constant.254.clone) | copy-start | bytes 49156
  504.9 36.0 %all-to-all-start.1 = ((f32[8,5,128,128]{3,2,1,0:T(8,128)}), f32[8,5,128,128]{3,2,1,0:T(8,128)S(1)}, u32[]{:S(2)}, u32[]{:S(2)}) async-start(f32[8,5,128,128]{3,2,1,0:T(8,128)} %column_inverse.4), calls=%async_computation.1 | async-start | bytes 5242880 | tf_op jit(solution)/shard_map/all_to_all | solution.py:651
  542.4 36.7 %all-to-all-start.5 = ((f32[8,5,128,128]{3,2,1,0:T(8,128)}), f32[8,5,128,128]{3,2,1,0:T(8,128)}, u32[]{:S(2)}, u32[]{:S(2)}) async-start(f32[8,5,128,128]{3,2,1,0:T(8,128)} %column_inverse.6), calls=%async_computation.5 | async-start | bytes 5242880 | tf_op jit(solution)/shard_map/all_to_all | solution.py:651
  579.2 35.8 %all-to-all-start.7 = ((f32[8,5,128,128]{3,2,1,0:T(8,128)}), f32[8,5,128,128]{3,2,1,0:T(8,128)S(1)}, u32[]{:S(2)}, u32[]{:S(2)}) async-start(f32[8,5,128,128]{3,2,1,0:T(8,128)} %column_inverse.7), calls=%async_computation.7 | async-start | bytes 5242880 | tf_op jit(solution)/shard_map/all_to_all | solution.py:651
  608.6 12.3 %copy-start.17 = (s32[1,2,256]{2,1,0:T(2,128)S(1)}, s32[1,2,256]{2,1,0:T(2,128)}, u32[]{:S(2)}) copy-start(s32[1,2,256]{2,1,0:T(2,128)} %param.81) | copy-start | bytes 6148
  608.6 13.3 %copy-start.18 = (s32[1,256]{1,0:T(1,128)S(1)}, s32[1,256]{1,0:T(1,128)}, u32[]{:S(2)}) copy-start(s32[1,256]{1,0:T(1,128)} %param.79) | copy-start | bytes 3076
  608.6 14.5 %copy-start.16 = (s32[1,256,1]{1,2,0:T(1,128)S(1)}, s32[1,256,1]{1,2,0:T(1,128)}, u32[]{:S(2)}) copy-start(s32[1,256,1]{1,2,0:T(1,128)} %param.82) | copy-start | bytes 3076
  616.5 36.7 %all-to-all-start.3 = ((f32[8,5,128,128]{3,2,1,0:T(8,128)}), f32[8,5,128,128]{3,2,1,0:T(8,128)}, u32[]{:S(2)}, u32[]{:S(2)}) async-start(f32[8,5,128,128]{3,2,1,0:T(8,128)} %column_inverse.5), calls=%async_computation.3 | async-start | bytes 5242880 | tf_op jit(solution)/shard_map/all_to_all | solution.py:651
  624.2 56.6 %copy-start.19 = (s32[1,256]{1,0:T(1,128)S(1)}, s32[1,256]{1,0:T(1,128)}, u32[]{:S(2)}) copy-start(s32[1,256]{1,0:T(1,128)} %param.80) | copy-start | bytes 3076
  675.3 8.7 %collective-permute-start = (f32[6,2,4096]{2,1,0:T(2,128)S(1)}, f32[6,2,4096]{2,1,0:T(2,128)S(1)}, u32[]{:S(2)}, u32[]{:S(2)}) collective-permute-start(f32[6,2,4096]{2,1,0:T(2,128)S(1)} %get-tuple-element.23), channel_id=1, source_target_pairs={{0,1},{1,2},{2,3},{3,4},{4,5},{5,6},{6,7},{7,8},{8,9},{9,10},{10,1... | collective-permute-start | bytes 589832 | tf_op jit(solution)/shard_map/ppermute | solution.py:698
  675.4 8.7 %collective-permute-start.1 = (f32[6,2,4096]{2,1,0:T(2,128)S(1)}, f32[6,2,4096]{2,1,0:T(2,128)S(1)}, u32[]{:S(2)}, u32[]{:S(2)}) collective-permute-start(f32[6,2,4096]{2,1,0:T(2,128)S(1)} %get-tuple-element.24), channel_id=1, source_target_pairs={{1,0},{2,1},{3,2},{4,3},{5,4},{6,5},{7,6},{8,7},{9,8},{10,9},{11,1... | collective-permute-start | bytes 589832 | tf_op jit(solution)/shard_map/ppermute | solution.py:699
  (5 other events, 8.9 us)
Sparse Core Ops, SparseCore 0:
  174.1 297.7 all-reduce.2

commit v2 on v1

--- a/solution.py
+++ b/solution.py
@@ -15,6 +15,7 @@
 HALF = 64
 SLOTS = 16
 FIELDS = 5
+EDGE_STEP = 2
 HIGH = lax.Precision.HIGHEST
 VMEM_LIMIT = 56 * 1024 * 1024
 
@@ -117,7 +118,9 @@
 
 
 def dot3(left, right):
-    return mm(left[0], right[0]) + mm(left[0], right[1]) + mm(left[1], right[0])
+    rows = left[0].shape[0]
+    both = mm(jnp.concatenate(left, axis=0), right[0])
+    return both[:rows] + both[rows:] + mm(left[0], right[1])
 
 
 def rotate(value):
@@ -218,8 +221,9 @@
 
 
 def column_forward_kernel(
-    grid_len, depth_ref, x_ref, kx_ref, kh, kl, ca, sa, cw, sw, out_ref, u_ref, c_ref, s_ref
+    grid_len, depth_ref, x_ref, kx_ref, kh, kl, ca, sa, cw, sw, low_ref, high_ref, *scratch
 ):
+    u_ref, c_ref, s_ref = scratch
     outer_len = grid_len // RADIX
     table = (kh[...], kl[...])
 
@@ -248,7 +252,10 @@
     s_ref[...] = sa[...]
     top, thick = depth_ref[0], depth_ref[1]
 
-    def second(k1, carry):
+    middle = outer_len // 2
+
+    def second(out_ref, start, step, carry):
+        k1 = start + step
         cosine, sine = c_ref[...], s_ref[...]
         table = split(jnp.concatenate([cosine, sine], axis=1))
         c_ref[...] = cosine * cw[...] - sine * sw[...]
@@ -259,10 +266,13 @@
         full_y, _ = wave_y(k1, (RADIX, RADIX), grid_len)
         magnitude = jnp.sqrt(kx_ref[...] * kx_ref[...] + full_y * full_y)
         scale = (1.0 - jnp.exp(-magnitude * thick)) * jnp.exp(-magnitude * top)
-        out_ref[rows, :] = result * (scale * (2.0 * math.pi / (grid_len * grid_len)))
+        out_ref[pl.ds(pl.multiple_of(step * RADIX, RADIX), RADIX), :] = result * (
+            scale * (2.0 * math.pi / (grid_len * grid_len))
+        )
         return carry
 
-    lax.fori_loop(0, outer_len, second, 0, unroll=2)
+    lax.fori_loop(0, middle, functools.partial(second, low_ref, 0), 0, unroll=2)
+    lax.fori_loop(0, middle, functools.partial(second, high_ref, middle), 0, unroll=2)
 
 
 def column_forward(block, wave_x, depths):
@@ -282,8 +292,8 @@
         functools.partial(column_forward_kernel, grid_len),
         in_specs=[pl.BlockSpec(memory_space=pltpu.SMEM)]
         + [pl.BlockSpec(memory_space=pltpu.VMEM)] * (2 + len(tables)),
-        out_specs=pl.BlockSpec(memory_space=pltpu.VMEM),
-        out_shape=jax.ShapeDtypeStruct(block.shape, jnp.float32),
+        out_specs=[pl.BlockSpec(memory_space=pltpu.VMEM)] * 2,
+        out_shape=[jax.ShapeDtypeStruct((grid_len // 2, RADIX), jnp.float32)] * 2,
         scratch_shapes=[
             pltpu.VMEM((grid_len, RADIX), jnp.float32),
             pltpu.VMEM(square, jnp.float32),
@@ -291,7 +301,7 @@
         ],
         compiler_params=pltpu.CompilerParams(vmem_limit_bytes=VMEM_LIMIT),
         cost_estimate=pl.CostEstimate(
-            flops=24 * grid_len * RADIX * 256,
+            flops=100 * grid_len * RADIX * 256,
             bytes_accessed=8 * grid_len * RADIX,
             transcendentals=2 * grid_len * RADIX,
         ),
@@ -300,30 +310,45 @@
 
 
 def column_inverse_kernel(
-    grid_len, tile_rows, special, flag_ref, s_in, kx_ref, kxo_ref, bh, bl, ca, sa, cw, sw, *refs
+    grid_len, tile_rows, start, count, special, added, keys, flag_ref, kx_ref, kxo_ref, *refs
 ):
-    if special:
-        edge_ref, out_ref, v_ref, c_ref, s_ref = refs
-    else:
-        out_ref, v_ref, c_ref, s_ref = refs
-    outer_len = grid_len // RADIX
+    moves = [refs[0:1]]
+    at = 1
+    for group in keys:
+        moves.append(refs[at : at + len(group)])
+        at += len(group)
+    refs, (held, arrived) = refs[at:-2], refs[-2:]
+    for slot, (group, sources) in enumerate(zip(((),) + keys, moves)):
+        for position, source in enumerate(sources):
+            fetch = pltpu.make_async_copy(source, held.at[slot], arrived.at[slot])
+            if slot == 0:
+                fetch.start()
+            elif position == 0:
+                others = [flag_ref[1] != key for key in group[1:]]
+                pl.when(functools.reduce(jnp.logical_and, others, flag_ref[1] >= 0))(fetch.start)
+            else:
+                pl.when(flag_ref[1] == group[position])(fetch.start)
+    bh, bl, ca, sa, cw, sw = refs[:6]
+    edge_ref = refs[6] if special else None
+    sum_ref = refs[6 + special] if added else None
+    out_ref, v_ref, c_ref, s_ref = refs[6 + special + added :]
     here = bh.shape[0] // 8
     c_ref[...] = ca[...]
     s_ref[...] = sa[...]
 
-    def first(k1, carry):
+    def first(step, carry):
         cosine, sine = c_ref[...], s_ref[...]
         table = split(jnp.concatenate([cosine, sine], axis=1))
         c_ref[...] = cosine * cw[...] - sine * sw[...]
         s_ref[...] = sine * cw[...] + cosine * sw[...]
-        rows = pl.ds(pl.multiple_of(k1 * RADIX, RADIX), RADIX)
-        full_y, odd_y = wave_y(k1, (RADIX, RADIX), grid_len)
+        full_y, odd_y = wave_y(start + step, (RADIX, RADIX), grid_len)
         full_x, odd_x = kx_ref[...], kxo_ref[...]
         squared = full_x * full_x + full_y * full_y
         safe = jnp.where(squared > 0.0, squared, 1.0)
         root = lax.rsqrt(safe)
         inverse = root * root
-        value = s_in[rows, :]
+        rows = pl.ds(pl.multiple_of(step * RADIX, RADIX), RADIX)
+        value = held[0, rows, :] + held[1, rows, :] + held[2, rows, :]
         turned = rotate(value)
         coef_xx = -full_x * full_x * inverse
         coef_xy = -odd_x * odd_y * inverse
@@ -350,13 +375,15 @@
         v_ref[rows, :] = dot3(table, split(data))
         return carry
 
-    lax.fori_loop(0, outer_len, first, 0)
+    for slot, sources in enumerate(moves):
+        pltpu.make_async_copy(sources[0], held.at[slot], arrived.at[slot]).wait()
+    lax.fori_loop(0, count, first, 0)
     both = jnp.concatenate([bh[...], bl[...]], axis=0)
     span = 8 * here
 
     def second(group, carry):
         data = jnp.concatenate(
-            [v_ref[pl.ds(k1 * RADIX + group * 8, 8), :] for k1 in range(outer_len)], axis=0
+            [v_ref[pl.ds(k1 * RADIX + group * 8, 8), :] for k1 in range(count)], axis=0
         )
         turned = jnp.concatenate(
             [rotate(data[:, RADIX * c : RADIX * (c + 1)]) for c in range(FIELDS)], axis=1
@@ -370,6 +397,8 @@
             dest = a * per_row + (group * 8) // tile_rows
             for c in range(FIELDS):
                 piece = result[8 * a : 8 * a + 8, RADIX * c : RADIX * (c + 1)]
+                if added:
+                    piece = piece + sum_ref[dest, c, pl.ds(row, 8), :]
                 if special:
                     lane = lax.broadcasted_iota(jnp.int32, piece.shape, 1)
                     edge = edge_ref[c, pl.ds(a * RADIX + group * 8, 8), :]
@@ -381,40 +410,66 @@
     lax.fori_loop(0, RADIX // 8, second, 0)
 
 
-def column_inverse(block, wave_x, odd_x, share, flag, edge, wide_count, tile_rows):
-    grid_len = block.shape[0]
+def column_inverse(part, start, wave_x, odd_x, place, edge, partial_sum, sizes):
+    grid_len, wide_count, tile_rows = sizes
+    flag, row_start, row_share = place
+    piece, below, above = part
+    count = piece.shape[0] // RADIX
+    moved = [piece, *below.values(), *above.values()]
+    outer_len = grid_len // RADIX
     alpha = angles(np.arange(RADIX), np.arange(RADIX), RADIX)
     beta = 2.0 * math.pi * np.arange(RADIX)[:, None] / grid_len * np.ones((1, RADIX))
-    tables = (
+    alpha = alpha + start * beta
+    kron = column_kron(outer_len, 1.0)
+    chosen = np.arange(start * 8, (start + count) * 8)
+    kron = kron[:, np.concatenate([chosen, chosen + 8 * outer_len])]
+    share = [
+        lax.dynamic_slice_in_dim(item, row_start * 8, row_share * 8, 0) for item in np_split(kron)
+    ]
+    tables = [
         *share,
         f32(np.cos(alpha)),
         f32(np.sin(alpha)),
         f32(np.cos(beta)),
         f32(np.sin(beta)),
-    )
-    if edge is not None:
-        tables = tables + (edge,)
+    ]
+    extra = [item for item in (edge, partial_sum) if item is not None]
+    operands = [*tables, *extra]
+    plain = [pl.BlockSpec(memory_space=pltpu.VMEM)]
     square = (RADIX, RADIX)
     out_shape = (wide_count, FIELDS, tile_rows, RADIX)
     return pl.pallas_call(
-        functools.partial(column_inverse_kernel, grid_len, tile_rows, edge is not None),
+        functools.partial(
+            column_inverse_kernel,
+            grid_len,
+            tile_rows,
+            start,
+            count,
+            int(edge is not None),
+            int(partial_sum is not None),
+            (tuple(below), tuple(above)),
+        ),
         in_specs=[pl.BlockSpec(memory_space=pltpu.SMEM)]
-        + [pl.BlockSpec(memory_space=pltpu.VMEM)] * (3 + len(tables)),
+        + plain * 2
+        + [pl.BlockSpec(memory_space=pl.ANY)] * len(moved)
+        + plain * len(operands),
         out_specs=pl.BlockSpec(memory_space=pltpu.VMEM),
         out_shape=jax.ShapeDtypeStruct(out_shape, jnp.float32),
         scratch_shapes=[
-            pltpu.VMEM((grid_len, FIELDS * RADIX), jnp.float32),
+            pltpu.VMEM((count * RADIX, FIELDS * RADIX), jnp.float32),
             pltpu.VMEM(square, jnp.float32),
             pltpu.VMEM(square, jnp.float32),
+            pltpu.VMEM((3, count * RADIX, RADIX), jnp.float32),
+            pltpu.SemaphoreType.DMA((3,)),
         ],
         compiler_params=pltpu.CompilerParams(vmem_limit_bytes=VMEM_LIMIT),
         cost_estimate=pl.CostEstimate(
-            flops=FIELDS * 18 * grid_len * RADIX * 256,
-            bytes_accessed=4 * (grid_len * RADIX + math.prod(out_shape)),
-            transcendentals=grid_len * RADIX,
+            flops=FIELDS * 45 * count * RADIX * RADIX * 256,
+            bytes_accessed=4 * (count * RADIX * RADIX + math.prod(out_shape)),
+            transcendentals=count * RADIX * RADIX,
         ),
         name="column_inverse",
-    )(flag, block, wave_x, odd_x, *tables)
+    )(flag, wave_x, odd_x, *moved, *operands)
 
 
 def row_inverse_kernel(chunks, *refs):
@@ -527,19 +582,19 @@
 
 
 def interpolate(gradient, halo, weight_y, col_ids, weight_x, placement):
-    fields, rows, grid_len = gradient.shape
+    _, rows, grid_len = gradient.shape
     samples, slot_total = placement.shape
     small = (weight_y, col_ids, weight_x, placement)
     return pl.pallas_call(
         interpolate_kernel,
-        grid=(fields,),
+        grid=(FIELDS,),
         in_specs=[
             pl.BlockSpec((1, rows, grid_len), lambda i: (i, 0, 0)),
             pl.BlockSpec((1, 8, grid_len), lambda i: (i, 0, 0)),
         ]
         + [full_spec(item.shape) for item in small],
         out_specs=pl.BlockSpec((1, 1, slot_total), lambda i: (i, 0, 0)),
-        out_shape=jax.ShapeDtypeStruct((fields, 1, slot_total), jnp.float32),
+        out_shape=jax.ShapeDtypeStruct((FIELDS, 1, slot_total), jnp.float32),
         scratch_shapes=[pltpu.VMEM((samples, grid_len), jnp.float32)],
         compiler_params=pltpu.CompilerParams(vmem_limit_bytes=VMEM_LIMIT),
         name="interpolate",
@@ -634,8 +689,43 @@
     return weights, base[:, None] - 1 + taps
 
 
-def depth_sum(blocks):
-    return [lax.psum(block, "depth") for block in blocks]
+def choose(which, candidates):
+    picked = None
+    for key, value in candidates.items():
+        picked = value if picked is None else jnp.where(which == key, value, picked)
+    return picked
+
+
+def depth_scan(pieces, jobs, total, aside):
+    count = lax.axis_size("depth")
+    here = lax.axis_index("depth")
+    up = [(i, i + 1) for i in range(count - 1)]
+    down = [(i + 1, i) for i in range(count - 1)]
+    from_below, from_above = [], []
+
+    def complete(index):
+        below = {d: from_below[index + d - 1] for d in range(1, count)}
+        above = {count - 1 - d: from_above[index + d - 1] for d in range(1, count)}
+        return pieces[index], below, above
+
+    for step in range(total + count - 2):
+        live = [d for d in range(count - 1) if 0 <= step - d < total]
+        rising = choose(here, {d: pieces[step - d] for d in live})
+        falling = choose(here, {count - 1 - d: pieces[step - d] for d in live})
+        if step:
+            rising, falling = rising + from_below[-1], falling + from_above[-1]
+        work = [jobs[step]] if step in jobs else []
+        if step == aside[0]:
+            work.append(aside[1:])
+        keys = [key for _, key in work]
+        rising, falling, keys = lax.optimization_barrier((rising, falling, keys))
+        below = lax.ppermute(rising, "depth", up)
+        above = lax.ppermute(falling, "depth", down)
+        results = [task(key, complete) for (task, _), key in zip(work, keys)]
+        below, above, _ = lax.optimization_barrier((below, above, results))
+        from_below.append(below)
+        from_above.append(above)
+    return complete
 
 
 def per_device(density, layer_top, layer_thick, sample_row, sample_col, sample_frac, sample_owner):
@@ -670,36 +760,55 @@
     edge = edge_forward(
         jnp.stack([columns[0][:, 0], columns[0][:, HALF]]), layer_top[0], layer_thick[0]
     )
-    summed = depth_sum([column_forward(c, w, depths) for c, w in zip(columns, waves)])
+    edge = lax.psum(edge, "depth")
     row_share = outer_len // depth_count
     row_start = depth_id * row_share
-    edge = edge_inverse(lax.psum(edge, "depth"), row_start, row_share)
-    back = np_split(column_kron(outer_len, 1.0))
-    share = [lax.dynamic_slice_in_dim(item, row_start * 8, row_share * 8, 0) for item in back]
-    flag = wide_id.astype(jnp.int32).reshape(1)
-    blocks = []
+    place = (jnp.stack([wide_id, depth_id]).astype(jnp.int32), row_start, row_share)
+    sizes = (grid_len, wide_count, tile_rows)
+    pieces, blocks, partial_sums, edges = [], {}, {}, []
+
+    def forward_job(chunk, wave, complete):
+        pieces.extend(column_forward(columns[chunk], wave, depths))
+        return pieces[-1]
+
+    def edge_job(key, complete):
+        edges.append(edge_inverse(key, row_start, row_share))
+        return edges[0]
+
+    def early_job(chunk, wave, complete):
+        item = column_inverse(complete(2 * chunk), 0, wave, wave, place, None, None, sizes)
+        partial_sums[chunk] = item
+        return item
+
+    def late_job(chunk, wave, complete):
+        part = complete(2 * chunk + 1)
+        special = edges[0] if chunk == 0 else None
+        item = column_inverse(
+            part, outer_len // 2, wave, wave, place, special, partial_sums[chunk], sizes
+        )
+        blocks[chunk] = exchange(item)
+        return item
+
+    forward_job(0, waves[0], None)
+    jobs = {}
+    last = chunks - 1
     for chunk in range(chunks):
-        item = column_inverse(
-            summed[chunk],
-            waves[chunk],
-            waves[chunk],
-            share,
-            flag,
-            edge if chunk == 0 else None,
-            wide_count,
-            tile_rows,
-        )
-        blocks.append(exchange(item))
+        if chunk:
+            jobs[chunk - 1] = (functools.partial(forward_job, chunk), waves[chunk])
+        jobs[2 * chunk + depth_count - 1] = (functools.partial(early_job, chunk), waves[chunk])
+        if chunk < last:
+            jobs[2 * chunk + depth_count] = (functools.partial(late_job, chunk), waves[chunk])
+    complete = depth_scan(pieces, jobs, 2 * chunks, (EDGE_STEP, edge_job, edge))
+    late_job(last, waves[last], complete)
+    blocks = [blocks[chunk] for chunk in range(chunks)]
     gradient = row_inverse(blocks, grid_len)
 
     tiles = depth_count * wide_count
     forward = [(i, (i + 1) % tiles) for i in range(tiles)]
     backward = [(target, source) for source, target in forward]
-    low = lax.ppermute(gradient[:, tile_rows - 2 :], ("depth", "wide"), forward)
-    high = lax.ppermute(gradient[:, :2], ("depth", "wide"), backward)
-    halo = jnp.concatenate(
-        [low, high, jnp.zeros((FIELDS + 1, 4, grid_len), jnp.float32)], axis=1
-    )
+    low = lax.ppermute(gradient[:FIELDS, tile_rows - 2 :], ("depth", "wide"), forward)
+    high = lax.ppermute(gradient[:FIELDS, :2], ("depth", "wide"), backward)
+    halo = jnp.concatenate([low, high, jnp.zeros((FIELDS, 4, grid_len), jnp.float32)], axis=1)
 
     taps_y, offset_y = tap_weights(sample_frac[0, 0])
     taps_x, offset_x = tap_weights(sample_frac[0, 1])
@@ -724,9 +833,10 @@
         jnp.float32
     )
     outgoing = interpolate(gradient, halo, weight_y, col_ids, taps_x, placement)
-    outgoing = outgoing.reshape(FIELDS + 1, wide_count, capacity)
+    outgoing = outgoing.reshape(FIELDS, wide_count, capacity)
     arrived = lax.all_to_all(outgoing, "wide", split_axis=1, concat_axis=1, tiled=True)
-    return (gradient, arrived.reshape(FIELDS + 1, 1, slot_total))
+    arrived = arrived.reshape(FIELDS, 1, slot_total)
+    return (gradient, jnp.concatenate([arrived, -(arrived[0:1] + arrived[3:4])]))
 
 
 def solution(mesh):

time: 720 us -> 518 us (0.72)
  waiting for transfers between devices: 371 us -> 124 us
  blocking collectives: 68.9 us -> 7.09 us
  starting transfers between devices: 29.7 us -> 86.5 us
  Pallas kernels: 209 us -> 235 us
  other arithmetic: 7.83 us -> 25.1 us
    psum x1, waiting for transfers between devices: 296 us -> 0.01 us  [per_device(): edge = lax.psum(edge, 'depth')]
    ppermute x2 -> x22, waiting for transfers between devices: 2.54 us -> 67.1 us  [the longest x10 36.9 us: depth_scan(): above = lax.ppermute(falling, 'depth', down)]
    all_to_all x2 -> x0, blocking collectives: 61.8 us -> none  [exchange(): lax.all_to_all(block, 'wide', split_axis=0, concat_axis=0, tiled=True)]
    ppermute x2 -> x22, starting transfers between devices: 5.39 us -> 50.8 us  [the longest x10 32.3 us: depth_scan(): below = lax.ppermute(rising, 'depth', up)]
    pallas_call x4 -> x8, Pallas kernels: 104 us -> 134 us  [column_inverse(): pl.pallas_call(functools.partial(column_inverse_kernel, grid_len, tile_ro...]
    add x0 -> x9, other arithmetic: none -> 16.2 us  [depth_scan(): rising, falling = (rising + from_below[-1], falling + from_above[-1])]
    all_to_all x6 -> x8, waiting for transfers between devices: 71.7 us -> 57.4 us  [exchange(): lax.all_to_all(block, 'wide', split_axis=0, concat_axis=0, tiled=True)]
    all_to_all x6 -> x8, starting transfers between devices: 24.3 us -> 35.7 us  [exchange(): lax.all_to_all(block, 'wide', split_axis=0, concat_axis=0, tiled=True)]
  transfers between devices with their start and end apart: 9 -> 31, of which waited for: 7 -> 22; matrix products, arithmetic and copies ran while one was open for 1% -> 7% of each run, Pallas kernels for 16% -> 35%
where the time goes in v2:
time: 518 us; the launch traced here: 516 us
  Pallas kernels  235 us (45%)
  waiting for transfers between devices  124 us (24%)
  starting transfers between devices  86.5 us (17%)
  other arithmetic  25.1 us (5%)
  local copies, waits for them, and re-layouts  16.2 us (3%)
  between operations  16.1 us (3%)
  blocking collectives  7.09 us (1%)
  matrix products  5.69 us (1%)
    pallas_call x8, Pallas kernels, column_inverse(): pl.pallas_call(functools.partial(column_inverse_kernel, grid_len, tile_ro...  134 us
    all_to_all x8, waiting for transfers between devices, exchange(): lax.all_to_all(block, 'wide', split_axis=0, concat_axis=0, tiled=True)  57.4 us
    pallas_call x4, Pallas kernels, column_forward(): pl.pallas_call(functools.partial(column_forward_kernel, grid_len), in_spe...  48.1 us
    ppermute x10, waiting for transfers between devices, depth_scan(): above = lax.ppermute(falling, 'depth', down)  36.9 us
    all_to_all x8, starting transfers between devices, exchange(): lax.all_to_all(block, 'wide', split_axis=0, concat_axis=0, tiled=True)  35.7 us
    ppermute x10, starting transfers between devices, depth_scan(): below = lax.ppermute(rising, 'depth', up)  32.3 us
    ppermute x10, waiting for transfers between devices, depth_scan(): below = lax.ppermute(rising, 'depth', up)  27.9 us
    pallas_call x1, Pallas kernels, row_inverse(): pl.pallas_call(functools.partial(row_inverse_kernel, chunks), grid=(rows...  20.6 us
  transfers between devices with their start and end apart: 31, of which 22 were waited for; matrix products, arithmetic and copies ran while one was open for 7% of the time, Pallas kernels for 35%

profile of v2, /device:TPU:0, one launch (start us, length us, event | category | flops | bytes accessed | tf_op | source)
XLA Modules:
  0.0 516.1 jit_solution(6185682784086737421)
XLA Ops:
  7.2 17.0 %row_forward.1 = (f32[8,512,128]{2,1,0:T(8,128)}, f32[8,512,128]{2,1,0:T(8,128)}, f32[8,512,128]{2,1,0:T(8,128)}, f32[8,512,128]{2,1,0:T(8,128)}) custom-call(f32[512,4096]{1,0:T(8,128)} %bitcast.91, bf16[256,256]{1,0:T(8,128)(2,1)} %constant.242.clone.kh, bf16[256,256]{1,0:T(8,128)(2,1)} %constant.243.clone.kl, f32[256,256]{1,0:T(8,128)} %constant.244.clone.base, ...), custom_call_target="tpu_custom_call" | custom-call | flops 6442450944 | bytes 16777216 | tf_op jit(solution)/shard_map/row_forward/pallas_call | solution.py:194
  24.2 5.2 %all-to-all-start.1 = ((f32[8,512,128]{2,1,0:T(8,128)}), f32[8,512,128]{2,1,0:T(8,128)S(1)}, u32[]{:S(2)}, u32[]{:S(2)}) async-start(f32[8,512,128]{2,1,0:T(8,128)} %get-tuple-element.66), calls=%async_computation.1 | async-start | bytes 4194304 | tf_op jit(solution)/shard_map/all_to_all | solution.py:741
  36.4 19.6 %all-to-all-done.1 = f32[8,512,128]{2,1,0:T(8,128)S(1)} async-done(((f32[8,512,128]{2,1,0:T(8,128)}), f32[8,512,128]{2,1,0:T(8,128)S(1)}, u32[]{:S(2)}, u32[]{:S(2)}) %all-to-all-start.1) | async-done | bytes 2097184 | tf_op jit(solution)/shard_map/all_to_all | solution.py:741
  60.4 11.9 %column_forward.4 = (f32[2048,128]{1,0:T(8,128)}, f32[2048,128]{1,0:T(8,128)}) custom-call(f32[2]{0:T(128)} %pad_maximum_fusion.5.depth_ref, f32[4096,128]{1,0:T(8,128)} %bitcast.73, f32[1,128]{1,0:T(1,128)} %convert_multiply_fusion.3.kx_ref.kxo_ref, bf16[256,512]{1,0:T(8,128)(2,1)} %constant.255.clone.kh, bf16[256,512]{1,0:T(8,128)(2,1)} %constant.256.clone.kl, ...), custom_call_target="tpu_custom_call" | custom-call | flops 13421772800 | bytes 4194304 | tf_op jit(solution)/shard_map/column_forward/pallas_call | solution.py:291
  91.4 12.1 %column_forward.5 = (f32[2048,128]{1,0:T(8,128)}, f32[2048,128]{1,0:T(8,128)}) custom-call(f32[2]{0:T(128)} %pad_maximum_fusion.5.depth_ref, f32[4096,128]{1,0:T(8,128)} %bitcast.3.x_ref, f32[1,128]{1,0:T(1,128)} %get-tuple-element.108.kx_ref.kxo_ref, bf16[256,512]{1,0:T(8,128)(2,1)} %constant.255.clone.kh, bf16[256,512]{1,0:T(8,128)(2,1)} %constant.256.clone.kl, ...), custom_call_target="tpu_custom_call" | custom-call | flops 13421772800 | bytes 4194304 | tf_op jit(solution)/shard_map/column_forward/pallas_call | solution.py:291
  122.4 12.0 %column_forward.6 = (f32[2048,128]{1,0:T(8,128)}, f32[2048,128]{1,0:T(8,128)}) custom-call(f32[2]{0:T(128)} %pad_maximum_fusion.5.depth_ref, f32[4096,128]{1,0:T(8,128)} %bitcast.5.x_ref, f32[1,128]{1,0:T(1,128)} %get-tuple-element.118.kx_ref.kxo_ref, bf16[256,512]{1,0:T(8,128)(2,1)} %constant.255.clone.kh, bf16[256,512]{1,0:T(8,128)(2,1)} %constant.256.clone.kl, ...), custom_call_target="tpu_custom_call" | custom-call | flops 13421772800 | bytes 4194304 | tf_op jit(solution)/shard_map/column_forward/pallas_call | solution.py:291
  155.0 12.1 %column_forward.7 = (f32[2048,128]{1,0:T(8,128)}, f32[2048,128]{1,0:T(8,128)}) custom-call(f32[2]{0:T(128)} %pad_maximum_fusion.5.depth_ref, f32[4096,128]{1,0:T(8,128)} %bitcast.16.x_ref, f32[1,128]{1,0:T(1,128)} %convert_multiply_fusion.kx_ref.kxo_ref, bf16[256,512]{1,0:T(8,128)(2,1)} %constant.255.clone.kh, bf16[256,512]{1,0:T(8,128)(2,1)} %constant.256.clone.kl, ...), custom_call_target="tpu_custom_call" | custom-call | flops 13421772800 | bytes 4194304 | tf_op jit(solution)/shard_map/column_forward/pallas_call | solution.py:291
  167.1 7.1 %collective-permute-done.4.refs_3_.refs_2_.refs_1_ = f32[2048,128]{1,0:T(8,128)} collective-permute-done((f32[2048,128]{1,0:T(8,128)}, f32[2048,128]{1,0:T(8,128)}, u32[]{:S(2)}, u32[]{:S(2)}) %collective-permute-start.4) | collective-permute-done | bytes 1048608 | tf_op jit(solution)/shard_map/ppermute | solution.py:722
  174.2 5.1 collective-permute-done.5.refs_6_.refs_5_.refs_4_
  185.3 16.2 %column_inverse.8.refs_14_ = f32[8,5,128,128]{3,2,1,0:T(8,128)} custom-call(s32[2]{0:T(128)} %pad_add_fusion.flag_ref, f32[1,128]{1,0:T(1,128)} %convert_multiply_fusion.3.kx_ref.kxo_ref, f32[1,128]{1,0:T(1,128)} %convert_multiply_fusion.3.kx_ref.kxo_ref, f32[2048,128]{1,0:T(8,128)} %get-tuple-element.74.refs_0_, f32[2048,128]{1,0:T(8,128)} %copy-done.14, ...), custom_call_target="tpu_custom_call" | custom-call | flops 15099494400 | bytes 3670016 | tf_op jit(solution)/shard_map/column_inverse/pallas_call | solution.py:441
  215.1 18.2 %column_inverse.9 = f32[8,5,128,128]{3,2,1,0:T(8,128)} custom-call(s32[2]{0:T(128)} %pad_add_fusion.flag_ref, f32[1,128]{1,0:T(1,128)} %convert_multiply_fusion.3.kx_ref.kxo_ref, f32[1,128]{1,0:T(1,128)} %convert_multiply_fusion.3.kx_ref.kxo_ref, f32[2048,128]{1,0:T(8,128)} %get-tuple-element.72.refs_0_, f32[2048,128]{1,0:T(8,128)} %collective-permute-done.2.refs_2_.refs_1_, ...), custom_call_target="tpu_custom_call" | custom-call | flops 15099494400 | bytes 3670016 | tf_op jit(solution)/shard_map/column_inverse/pallas_call | solution.py:441
  245.7 16.1 %column_inverse.10.refs_13_ = f32[8,5,128,128]{3,2,1,0:T(8,128)} custom-call(s32[2]{0:T(128)} %pad_add_fusion.flag_ref, f32[1,128]{1,0:T(1,128)} %get-tuple-element.108.kx_ref.kxo_ref, f32[1,128]{1,0:T(1,128)} %get-tuple-element.108.kx_ref.kxo_ref, f32[2048,128]{1,0:T(8,128)} %get-tuple-element.69.refs_0_, ...), custom_call_target="tpu_custom_call" | custom-call | flops 15099494400 | bytes 3670016 | tf_op jit(solution)/shard_map/column_inverse/pallas_call | solution.py:441
  261.9 5.4 %collective-permute-done.10.refs_3_.refs_2_.refs_1_ = f32[2048,128]{1,0:T(8,128)S(1)} collective-permute-done((f32[2048,128]{1,0:T(8,128)S(1)}, f32[2048,128]{1,0:T(8,128)S(1)}, u32[]{:S(2)}, u32[]{:S(2)}) %collective-permute-start.10) | collective-permute-done | bytes 1048608 | tf_op jit(solution)/shard_map/ppermute | solution.py:722
  276.9 17.2 %column_inverse.11 = f32[8,5,128,128]{3,2,1,0:T(8,128)} custom-call(s32[2]{0:T(128)} %pad_add_fusion.flag_ref, f32[1,128]{1,0:T(1,128)} %get-tuple-element.108.kx_ref.kxo_ref, f32[1,128]{1,0:T(1,128)} %get-tuple-element.108.kx_ref.kxo_ref, f32[2048,128]{1,0:T(8,128)} %get-tuple-element.70.refs_0_, f32[2048,128]{1,0:T(8,128)} %copy-done.19, ...), custom_call_target="tpu_custom_call" | custom-call | flops 15099494400 | bytes 3670016 | tf_op jit(solution)/shard_map/column_inverse/pallas_call | solution.py:441
  306.6 16.2 %column_inverse.12.refs_13_ = f32[8,5,128,128]{3,2,1,0:T(8,128)} custom-call(s32[2]{0:T(128)} %pad_add_fusion.flag_ref, f32[1,128]{1,0:T(1,128)} %get-tuple-element.118.kx_ref.kxo_ref, f32[1,128]{1,0:T(1,128)} %get-tuple-element.118.kx_ref.kxo_ref, f32[2048,128]{1,0:T(8,128)} %get-tuple-element.78.refs_0_, ...), custom_call_target="tpu_custom_call" | custom-call | flops 15099494400 | bytes 3670016 | tf_op jit(solution)/shard_map/column_inverse/pallas_call | solution.py:441
  340.2 17.2 %column_inverse.13 = f32[8,5,128,128]{3,2,1,0:T(8,128)} custom-call(s32[2]{0:T(128)} %pad_add_fusion.flag_ref, f32[1,128]{1,0:T(1,128)} %get-tuple-element.118.kx_ref.kxo_ref, f32[1,128]{1,0:T(1,128)} %get-tuple-element.118.kx_ref.kxo_ref, f32[2048,128]{1,0:T(8,128)} %get-tuple-element.81.refs_0_, f32[2048,128]{1,0:T(8,128)} %copy-done.18, ...), custom_call_target="tpu_custom_call" | custom-call | flops 15099494400 | bytes 3670016 | tf_op jit(solution)/shard_map/column_inverse/pallas_call | solution.py:441
  376.0 16.1 %column_inverse.14.refs_13_ = f32[8,5,128,128]{3,2,1,0:T(8,128)} custom-call(s32[2]{0:T(128)} %pad_add_fusion.flag_ref, f32[1,128]{1,0:T(1,128)} %convert_multiply_fusion.kx_ref.kxo_ref, f32[1,128]{1,0:T(1,128)} %convert_multiply_fusion.kx_ref.kxo_ref, f32[2048,128]{1,0:T(8,128)} %get-tuple-element.98.refs_0_, f32[2048,128]{1,0:T(8,128)} %copy-done.15, ...), custom_call_target="tpu_custom_call" | custom-call | flops 15099494400 | bytes 3670016 | tf_op jit(solution)/shard_map/column_inverse/pallas_call | solution.py:441
  392.3 5.1 collective-permute-done.19.refs_6_
  397.4 17.1 %column_inverse.15 = f32[8,5,128,128]{3,2,1,0:T(8,128)} custom-call(s32[2]{0:T(128)} %pad_add_fusion.flag_ref, f32[1,128]{1,0:T(1,128)} %convert_multiply_fusion.kx_ref.kxo_ref, f32[1,128]{1,0:T(1,128)} %convert_multiply_fusion.kx_ref.kxo_ref, f32[2048,128]{1,0:T(8,128)} %get-tuple-element.88.refs_0_, f32[2048,128]{1,0:T(8,128)} %copy-done.17, ...), custom_call_target="tpu_custom_call" | custom-call | flops 15099494400 | bytes 3670016 | tf_op jit(solution)/shard_map/column_inverse/pallas_call | solution.py:441
  424.1 28.8 %all-to-all-done.7.refs_3_ = f32[8,5,128,128]{3,2,1,0:T(8,128)} async-done(((f32[8,5,128,128]{3,2,1,0:T(8,128)}), f32[8,5,128,128]{3,2,1,0:T(8,128)}, u32[]{:S(2)}, u32[]{:S(2)}) %all-to-all-start.7) | async-done | bytes 2621472 | tf_op jit(solution)/shard_map/all_to_all | solution.py:741
  452.8 20.6 %row_inverse.1.g_ref = f32[6,128,4096]{2,1,0:T(8,128)} custom-call(f32[8,5,128,128]{3,2,1,0:T(8,128)} %all-to-all-done.4.refs_0_, f32[8,5,128,128]{3,2,1,0:T(8,128)} %all-to-all-done.5.refs_1_, f32[8,5,128,128]{3,2,1,0:T(8,128)} %copy-done.9, f32[8,5,128,128]{3,2,1,0:T(8,128)} %all-to-all-done.7.refs_3_, bf16[256,256]{1,0:T(8,128)(2,1)} %constant.272.clone.refs_4_, ...), custom_call_target="tpu_custom_call" | custom-call | flops 8053063680 | bytes 23068672 | tf_op jit(solution)/shard_map/row_inverse/pallas_call | solution.py:534
  474.9 5.3 %collective-permute-start.21 = (f32[5,2,4096]{2,1,0:T(2,128)S(1)}, f32[5,2,4096]{2,1,0:T(2,128)S(1)}, u32[]{:S(2)}, u32[]{:S(2)}) collective-permute-start(f32[5,2,4096]{2,1,0:T(2,128)S(1)} %get-tuple-element.137), channel_id=1, source_target_pairs={{1,0},{2,1},{3,2},{4,3},{5,4},{6,5},{7,6},{8,7},{9,8},{10,9},{11,1... | collective-permute-start | bytes 491528 | tf_op jit(solution)/shard_map/ppermute | solution.py:810
  484.3 14.9 %interpolate.1 = f32[5,1,512]{2,1,0:T(1,128)} custom-call(f32[6,128,4096]{2,1,0:T(8,128)} %row_inverse.1.g_ref, f32[5,8,4096]{2,1,0:T(8,128)} %maximum_maximum_fusion.halo_ref, f32[256,136]{1,0:T(8,128)} %copy.128.wy_ref, s32[256,4]{1,0:T(8,128)} %add_select_fusion.col_ref, f32[256,4]{1,0:T(8,128)} %get-tuple-element.162.wx_ref, f32[256,512]{1,0:T(8,128)} %fusion.5.place_ref), custom_call_target="tpu_custom_call" | custom-call | tf_op jit(solution)/shard_map/interpolate/pallas_call | solution.py:588
  500.1 7.1 %all_to_all.45 = f32[8,1,320]{2,1,0:T(1,128)S(1)} all-to-all(f32[8,1,320]{2,1,0:T(1,128)S(1)} %reshape.517), channel_id=1, replica_groups=mesh['depth'=4,'wide'=8] {'wide'}, dimensions={0} | all-to-all | bytes 20480 | tf_op jit(solution)/shard_map/all_to_all | solution.py:837
  (187 shorter events, 176.4 us)
Async XLA Ops:
  24.2 31.8 %all-to-all-start.1 = ((f32[8,512,128]{2,1,0:T(8,128)}), f32[8,512,128]{2,1,0:T(8,128)S(1)}, u32[]{:S(2)}, u32[]{:S(2)}) async-start(f32[8,512,128]{2,1,0:T(8,128)} %get-tuple-element.66), calls=%async_computation.1 | async-start | bytes 4194304 | tf_op jit(solution)/shard_map/all_to_all | solution.py:741
  56.0 31.0 %all-to-all-start = ((f32[8,512,128]{2,1,0:T(8,128)}), f32[8,512,128]{2,1,0:T(8,128)}, u32[]{:S(2)}, u32[]{:S(2)}) async-start(f32[8,512,128]{2,1,0:T(8,128)} %get-tuple-element.65), calls=%async_computation | async-start | bytes 4194304 | tf_op jit(solution)/shard_map/all_to_all | solution.py:741
  60.4 81.9 %all-reduce.2.cloned.1.call-start = ((), (), s32[]{:S(2)}) async-start(), calls=%async_computation.9 | async-start | bytes 131072 | tf_op jit(solution)/shard_map/psum | solution.py:763
  72.4 31.1 %collective-permute-start = (f32[2048,128]{1,0:T(8,128)}, f32[2048,128]{1,0:T(8,128)S(1)}, u32[]{:S(2)}, u32[]{:S(2)}) collective-permute-start(f32[2048,128]{1,0:T(8,128)} %get-tuple-element.74.refs_0_), channel_id=1, source_target_pairs={{0,8},{8,16},{16,24},{1,9},{9,17},{17,25},{2,10},{10,18},{18,26},{... | collective-permute-start | bytes 3145736 | tf_op jit(solution)/shard_map/ppermute | solution.py:722
  76.1 28.4 %collective-permute-start.1 = (f32[2048,128]{1,0:T(8,128)}, f32[2048,128]{1,0:T(8,128)}, u32[]{:S(2)}, u32[]{:S(2)}) collective-permute-start(f32[2048,128]{1,0:T(8,128)} %get-tuple-element.74.refs_0_), channel_id=1, source_target_pairs={{8,0},{16,8},{24,16},{9,1},{17,9},{25,17},{10,2},{18,10},{26,18},{... | collective-permute-start | bytes 3145736 | tf_op jit(solution)/shard_map/ppermute | solution.py:723
  87.0 31.0 %all-to-all-start.2 = ((f32[8,512,128]{2,1,0:T(8,128)}), f32[8,512,128]{2,1,0:T(8,128)}, u32[]{:S(2)}, u32[]{:S(2)}) async-start(f32[8,512,128]{2,1,0:T(8,128)} %get-tuple-element.71), calls=%async_computation.2 | async-start | bytes 4194304 | tf_op jit(solution)/shard_map/all_to_all | solution.py:741
  107.2 27.2 %collective-permute-start.2 = (f32[2048,128]{1,0:T(8,128)}, f32[2048,128]{1,0:T(8,128)}, u32[]{:S(2)}, u32[]{:S(2)}) collective-permute-start(f32[2048,128]{1,0:T(8,128)} %get-tuple-element.79), channel_id=1, source_target_pairs={{0,8},{8,16},{16,24},{1,9},{9,17},{17,25},{2,10},{10,18},{18,26},{... | collective-permute-start | bytes 3145736 | tf_op jit(solution)/shard_map/ppermute | solution.py:722
  111.7 27.4 %collective-permute-start.3 = (f32[2048,128]{1,0:T(8,128)}, f32[2048,128]{1,0:T(8,128)}, u32[]{:S(2)}, u32[]{:S(2)}) collective-permute-start(f32[2048,128]{1,0:T(8,128)} %get-tuple-element.80), channel_id=1, source_target_pairs={{8,0},{16,8},{24,16},{9,1},{17,9},{25,17},{10,2},{18,10},{26,18},{... | collective-permute-start | bytes 3145736 | tf_op jit(solution)/shard_map/ppermute | solution.py:723
  118.0 36.9 %all-to-all-start.3 = ((f32[8,512,128]{2,1,0:T(8,128)}), f32[8,512,128]{2,1,0:T(8,128)}, u32[]{:S(2)}, u32[]{:S(2)}) async-start(f32[8,512,128]{2,1,0:T(8,128)} %get-tuple-element.86), calls=%async_computation.3 | async-start | bytes 4194304 | tf_op jit(solution)/shard_map/all_to_all | solution.py:741
  153.5 25.8 %collective-permute-start.5 = (f32[2048,128]{1,0:T(8,128)}, f32[2048,128]{1,0:T(8,128)}, u32[]{:S(2)}, u32[]{:S(2)}) collective-permute-start(f32[2048,128]{1,0:T(8,128)} %get-tuple-element.85), channel_id=1, source_target_pairs={{8,0},{16,8},{24,16},{9,1},{17,9},{25,17},{10,2},{18,10},{26,18},{... | collective-permute-start | bytes 3145736 | tf_op jit(solution)/shard_map/ppermute | solution.py:723
  184.0 24.8 %collective-permute-start.7 = (f32[2048,128]{1,0:T(8,128)S(1)}, f32[2048,128]{1,0:T(8,128)S(1)}, u32[]{:S(2)}, u32[]{:S(2)}) collective-permute-start(f32[2048,128]{1,0:T(8,128)S(1)} %get-tuple-element.93), channel_id=1, source_target_pairs={{8,0},{16,8},{24,16},{9,1},{17,9},{25,17},{10,2},{18,10},{26,18},{... | collective-permute-start | bytes 3145736 | tf_op jit(solution)/shard_map/ppermute | solution.py:723
  210.5 27.4 %collective-permute-start.8 = (f32[2048,128]{1,0:T(8,128)}, f32[2048,128]{1,0:T(8,128)}, u32[]{:S(2)}, u32[]{:S(2)}) collective-permute-start(f32[2048,128]{1,0:T(8,128)} %get-tuple-element.99), channel_id=1, source_target_pairs={{0,8},{8,16},{16,24},{1,9},{9,17},{17,25},{2,10},{10,18},{18,26},{... | collective-permute-start | bytes 3145736 | tf_op jit(solution)/shard_map/ppermute | solution.py:722
  233.3 97.5 %all-to-all-start.4 = ((f32[8,5,128,128]{3,2,1,0:T(8,128)}), f32[8,5,128,128]{3,2,1,0:T(8,128)}, u32[]{:S(2)}, u32[]{:S(2)}) async-start(f32[8,5,128,128]{3,2,1,0:T(8,128)} %column_inverse.9), calls=%async_computation.4 | async-start | bytes 5242880 | tf_op jit(solution)/shard_map/all_to_all | solution.py:741
  239.8 27.4 %collective-permute-start.10 = (f32[2048,128]{1,0:T(8,128)S(1)}, f32[2048,128]{1,0:T(8,128)S(1)}, u32[]{:S(2)}, u32[]{:S(2)}) collective-permute-start(f32[2048,128]{1,0:T(8,128)S(1)} %get-tuple-element.103), channel_id=1, source_target_pairs={{0,8},{8,16},{16,24},{1,9},{9,17},{17,25},{2,10},{10,18},{18,26},{... | collective-permute-start | bytes 3145736 | tf_op jit(solution)/shard_map/ppermute | solution.py:722
  244.4 27.0 %collective-permute-start.11 = (f32[2048,128]{1,0:T(8,128)S(1)}, f32[2048,128]{1,0:T(8,128)S(1)}, u32[]{:S(2)}, u32[]{:S(2)}) collective-permute-start(f32[2048,128]{1,0:T(8,128)S(1)} %get-tuple-element.104), channel_id=1, source_target_pairs={{8,0},{16,8},{24,16},{9,1},{17,9},{25,17},{10,2},{18,10},{26,18},{... | collective-permute-start | bytes 3145736 | tf_op jit(solution)/shard_map/ppermute | solution.py:723
  273.2 24.8 %collective-permute-start.12 = (f32[2048,128]{1,0:T(8,128)}, f32[2048,128]{1,0:T(8,128)S(1)}, u32[]{:S(2)}, u32[]{:S(2)}) collective-permute-start(f32[2048,128]{1,0:T(8,128)} %get-tuple-element.109), channel_id=1, source_target_pairs={{0,8},{8,16},{16,24},{1,9},{9,17},{17,25},{2,10},{10,18},{18,26},{... | collective-permute-start | bytes 3145736 | tf_op jit(solution)/shard_map/ppermute | solution.py:722
  275.6 26.5 %collective-permute-start.13 = (f32[2048,128]{1,0:T(8,128)}, f32[2048,128]{1,0:T(8,128)S(1)}, u32[]{:S(2)}, u32[]{:S(2)}) collective-permute-start(f32[2048,128]{1,0:T(8,128)} %get-tuple-element.110), channel_id=1, source_target_pairs={{8,0},{16,8},{24,16},{9,1},{17,9},{25,17},{10,2},{18,10},{26,18},{... | collective-permute-start | bytes 3145736 | tf_op jit(solution)/shard_map/ppermute | solution.py:723
  305.3 25.5 %collective-permute-start.15 = (f32[2048,128]{1,0:T(8,128)S(1)}, f32[2048,128]{1,0:T(8,128)}, u32[]{:S(2)}, u32[]{:S(2)}) collective-permute-start(f32[2048,128]{1,0:T(8,128)S(1)} %get-tuple-element.114), channel_id=1, source_target_pairs={{8,0},{16,8},{24,16},{9,1},{17,9},{25,17},{10,2},{18,10},{26,18},{... | collective-permute-start | bytes 3145736 | tf_op jit(solution)/shard_map/ppermute | solution.py:723
  330.8 41.3 %all-to-all-start.5 = ((f32[8,5,128,128]{3,2,1,0:T(8,128)}), f32[8,5,128,128]{3,2,1,0:T(8,128)}, u32[]{:S(2)}, u32[]{:S(2)}) async-start(f32[8,5,128,128]{3,2,1,0:T(8,128)} %column_inverse.11), calls=%async_computation.5 | async-start | bytes 5242880 | tf_op jit(solution)/shard_map/all_to_all | solution.py:741
  336.7 25.1 %collective-permute-start.16 = (f32[2048,128]{1,0:T(8,128)S(1)}, f32[2048,128]{1,0:T(8,128)S(1)}, u32[]{:S(2)}, u32[]{:S(2)}) collective-permute-start(f32[2048,128]{1,0:T(8,128)S(1)} %get-tuple-element.119), channel_id=1, source_target_pairs={{0,8},{8,16},{16,24},{1,9},{9,17},{17,25},{2,10},{10,18},{18,26},{... | collective-permute-start | bytes 3145736 | tf_op jit(solution)/shard_map/ppermute | solution.py:722
  338.9 27.0 %collective-permute-start.17 = (f32[2048,128]{1,0:T(8,128)S(1)}, f32[2048,128]{1,0:T(8,128)S(1)}, u32[]{:S(2)}, u32[]{:S(2)}) collective-permute-start(f32[2048,128]{1,0:T(8,128)S(1)} %get-tuple-element.120), channel_id=1, source_target_pairs={{8,0},{16,8},{24,16},{9,1},{17,9},{25,17},{10,2},{18,10},{26,18},{... | collective-permute-start | bytes 3145736 | tf_op jit(solution)/shard_map/ppermute | solution.py:723
  370.8 26.6 %collective-permute-start.19 = (f32[2048,128]{1,0:T(8,128)}, f32[2048,128]{1,0:T(8,128)}, u32[]{:S(2)}, u32[]{:S(2)}) collective-permute-start(f32[2048,128]{1,0:T(8,128)} %get-tuple-element.124), channel_id=1, source_target_pairs={{8,0},{16,8},{24,16},{9,1},{17,9},{25,17},{10,2},{18,10},{26,18},{... | collective-permute-start | bytes 3145736 | tf_op jit(solution)/shard_map/ppermute | solution.py:723
  372.1 42.5 %all-to-all-start.6 = ((f32[8,5,128,128]{3,2,1,0:T(8,128)}), f32[8,5,128,128]{3,2,1,0:T(8,128)S(1)}, u32[]{:S(2)}, u32[]{:S(2)}) async-start(f32[8,5,128,128]{3,2,1,0:T(8,128)} %column_inverse.13), calls=%async_computation.6 | async-start | bytes 5242880 | tf_op jit(solution)/shard_map/all_to_all | solution.py:741
  416.2 36.7 %all-to-all-start.7 = ((f32[8,5,128,128]{3,2,1,0:T(8,128)}), f32[8,5,128,128]{3,2,1,0:T(8,128)}, u32[]{:S(2)}, u32[]{:S(2)}) async-start(f32[8,5,128,128]{3,2,1,0:T(8,128)} %column_inverse.15), calls=%async_computation.7 | async-start | bytes 5242880 | tf_op jit(solution)/shard_map/all_to_all | solution.py:741
  (42 other events, 497.7 us)
Sparse Core Ops, SparseCore 0:
  83.2 38.4 all-reduce.1

commit v3 on v2

--- a/solution.py
+++ b/solution.py
@@ -15,6 +15,8 @@
 HALF = 64
 SLOTS = 16
 FIELDS = 5
+GROUPS = ((0, 1, 2, 3, 4),)
+EVERY = tuple(range(FIELDS))
 EDGE_STEP = 2
 HIGH = lax.Precision.HIGHEST
 VMEM_LIMIT = 56 * 1024 * 1024
@@ -48,16 +50,19 @@
     return wave, part, upper, angles(np.arange(RADIX), freq, grid_len)
 
 
-def row_forward_tables(grid_len):
+def row_forward_tables(grid_len, slots):
     outer_len = grid_len // RADIX
-    theta = angles(np.arange(SLOTS), np.arange(outer_len), outer_len)
-    first = np.zeros((2 * SLOTS, outer_len))
+    stride = slots[1] - slots[0]
+    theta = angles(np.asarray(slots), np.arange(outer_len), outer_len)
+    first = np.zeros((2 * len(slots), outer_len))
     first[0::2] = np.cos(theta)
     first[1::2] = -np.sin(theta)
-    first[1] = np.cos(np.pi * np.arange(outer_len))
+    if slots[0] == 0:
+        first[1] = np.cos(np.pi * np.arange(outer_len))
     kron = np.kron(first, np.eye(8))
     wave, part = lane_order()
-    alpha = angles(np.arange(RADIX), wave, RADIX)
+    step = 2.0 * math.pi * np.arange(RADIX)[:, None] / grid_len * np.ones((1, 256))
+    alpha = angles(np.arange(RADIX), wave, RADIX) + slots[0] * step
     base = np.concatenate(
         [
             np.where(part == 0, np.cos(alpha), -np.sin(alpha)),
@@ -69,8 +74,7 @@
     top = np.where(upper, 0.0, table)
     top[:, (wave == 0) & (part == 1)] = np.cos(np.pi * np.arange(RADIX))[:, None]
     zero = np.concatenate([top, np.where(upper, table, 0.0)])
-    beta = 2.0 * math.pi * np.arange(RADIX)[:, None] / grid_len * np.ones((1, 256))
-    return kron, base, zero, np.cos(beta), np.sin(beta)
+    return kron, base, zero if slots[0] == 0 else base, np.cos(stride * step), np.sin(stride * step)
 
 
 def row_inverse_tables(grid_len):
@@ -128,9 +132,9 @@
     return jnp.where(lane < HALF, -1.0, 1.0) * pltpu.roll(value, HALF, 1)
 
 
-def row_forward_kernel(chunks, x_ref, kh, kl, base, zero, cw, sw, *refs):
-    outs = refs[:chunks]
-    th, tl, rot, u_ref = refs[chunks:]
+def row_forward_kernel(chunks, slots, x_ref, kh, kl, base, zero, cw, sw, *refs):
+    outs = refs[:-4]
+    th, tl, rot, u_ref = refs[-4:]
     rows = x_ref.shape[0]
     outer_len = x_ref.shape[1] // RADIX
 
@@ -138,7 +142,7 @@
     def _():
         th[0], tl[0] = split(zero[...])
         rot[...] = base[...]
-        for slot in range(1, SLOTS):
+        for slot in range(1, len(slots)):
             top, low = rot[0:RADIX, :], rot[RADIX:, :]
             rot[0:RADIX, :] = cw[...] * top - sw[...] * low
             rot[RADIX:, :] = cw[...] * low + sw[...] * top
@@ -160,8 +164,8 @@
         u_ref[pair] = dot3(table, split(jnp.concatenate(halves, axis=1)))
         return carry
 
-    lax.fori_loop(0, rows // 16, first, 0)
-    for slot in range(SLOTS):
+    lax.fori_loop(0, rows // 16, first, 0, unroll=min(2, rows // 16))
+    for slot in range(len(slots)):
         parts = []
         for part in range(2):
             at = 16 * slot + 8 * part
@@ -177,36 +181,37 @@
             )
         result = dot3(split(jnp.concatenate(parts, axis=1)), (th[slot], tl[slot]))
         for side in range(2):
-            block = 2 * slot + side
-            outs[block % chunks][block // chunks] = result[:, RADIX * side : RADIX * (side + 1)]
+            block = 2 * slots[slot] + side
+            outs[block % chunks % len(outs)][block // chunks] = result[:, RADIX * side : RADIX * (side + 1)]
 
 
 def full_spec(shape):
     return pl.BlockSpec(shape, lambda *_: (0,) * len(shape))
 
 
-def row_forward(field, wide_count):
+def row_forward(field, wide_count, slots):
     rows, grid_len = field.shape
     chunks = 2 * SLOTS // wide_count
+    made = min(chunks, 2) if len(slots) < SLOTS else chunks
     step = min(rows, 128)
-    kron, base, zero, cw, sw = row_forward_tables(grid_len)
+    kron, base, zero, cw, sw = row_forward_tables(grid_len, slots)
     tables = (*np_split(kron), f32(base), f32(zero), f32(cw), f32(sw))
     return pl.pallas_call(
-        functools.partial(row_forward_kernel, chunks),
+        functools.partial(row_forward_kernel, chunks, slots),
         grid=(rows // step,),
         in_specs=[pl.BlockSpec((step, grid_len), lambda i: (i, 0))]
         + [full_spec(item.shape) for item in tables],
-        out_specs=[pl.BlockSpec((wide_count, step, RADIX), lambda i: (0, i, 0))] * chunks,
-        out_shape=[jax.ShapeDtypeStruct((wide_count, rows, RADIX), jnp.float32)] * chunks,
+        out_specs=[pl.BlockSpec((wide_count, step, RADIX), lambda i: (0, i, 0))] * made,
+        out_shape=[jax.ShapeDtypeStruct((wide_count, rows, RADIX), jnp.float32)] * made,
         scratch_shapes=[
-            pltpu.VMEM((SLOTS, 256, 256), jnp.bfloat16),
-            pltpu.VMEM((SLOTS, 256, 256), jnp.bfloat16),
+            pltpu.VMEM((len(slots), 256, 256), jnp.bfloat16),
+            pltpu.VMEM((len(slots), 256, 256), jnp.bfloat16),
             pltpu.VMEM((256, 256), jnp.float32),
-            pltpu.VMEM((step // 16, 256, 256), jnp.float32),
+            pltpu.VMEM((step // 16, 16 * len(slots), 256), jnp.float32),
         ],
         compiler_params=pltpu.CompilerParams(vmem_limit_bytes=VMEM_LIMIT),
         cost_estimate=pl.CostEstimate(
-            flops=12 * rows * grid_len * 256, bytes_accessed=8 * rows * grid_len, transcendentals=0
+            flops=20 * len(slots) // SLOTS * rows * grid_len * 256, bytes_accessed=8 * rows * grid_len, transcendentals=0
         ),
         name="row_forward",
     )(field, *tables)
@@ -247,7 +252,7 @@
                 ]
         return carry
 
-    lax.fori_loop(0, RADIX // 16, first, 0)
+    lax.fori_loop(0, RADIX // 16, first, 0, unroll=4)
     c_ref[...] = ca[...]
     s_ref[...] = sa[...]
     top, thick = depth_ref[0], depth_ref[1]
@@ -271,8 +276,8 @@
         )
         return carry
 
-    lax.fori_loop(0, middle, functools.partial(second, low_ref, 0), 0, unroll=2)
-    lax.fori_loop(0, middle, functools.partial(second, high_ref, middle), 0, unroll=2)
+    lax.fori_loop(0, middle, functools.partial(second, low_ref, 0), 0, unroll=4)
+    lax.fori_loop(0, middle, functools.partial(second, high_ref, middle), 0, unroll=4)
 
 
 def column_forward(block, wave_x, depths):
@@ -310,8 +315,9 @@
 
 
 def column_inverse_kernel(
-    grid_len, tile_rows, start, count, special, added, keys, flag_ref, kx_ref, kxo_ref, *refs
+    grid_len, tile_rows, start, count, special, added, keys, fields, flag_ref, kx_ref, kxo_ref, *refs
 ):
+    keys = tuple(group for group in keys if group)
     moves = [refs[0:1]]
     at = 1
     for group in keys:
@@ -348,7 +354,9 @@
         root = lax.rsqrt(safe)
         inverse = root * root
         rows = pl.ds(pl.multiple_of(step * RADIX, RADIX), RADIX)
-        value = held[0, rows, :] + held[1, rows, :] + held[2, rows, :]
+        value = held[0, rows, :]
+        for slot in range(1, held.shape[0]):
+            value = value + held[slot, rows, :]
         turned = rotate(value)
         coef_xx = -full_x * full_x * inverse
         coef_xy = -odd_x * odd_y * inverse
@@ -369,15 +377,15 @@
             turned * coef_yy,
             -value * slope_y,
         ]
-        data = jnp.concatenate(
-            [jnp.concatenate(upper, axis=1), jnp.concatenate(lower, axis=1)], axis=0
-        )
+        upper = jnp.concatenate([upper[c] for c in fields], axis=1)
+        lower = jnp.concatenate([lower[c] for c in fields], axis=1)
+        data = jnp.concatenate([upper, lower], axis=0)
         v_ref[rows, :] = dot3(table, split(data))
         return carry
 
     for slot, sources in enumerate(moves):
         pltpu.make_async_copy(sources[0], held.at[slot], arrived.at[slot]).wait()
-    lax.fori_loop(0, count, first, 0)
+    lax.fori_loop(0, count, first, 0, unroll=8)
     both = jnp.concatenate([bh[...], bl[...]], axis=0)
     span = 8 * here
 
@@ -386,7 +394,7 @@
             [v_ref[pl.ds(k1 * RADIX + group * 8, 8), :] for k1 in range(count)], axis=0
         )
         turned = jnp.concatenate(
-            [rotate(data[:, RADIX * c : RADIX * (c + 1)]) for c in range(FIELDS)], axis=1
+            [rotate(data[:, RADIX * c : RADIX * (c + 1)]) for c in range(len(fields))], axis=1
         )
         high, low = split(jnp.concatenate([data, turned], axis=0))
         stacked = mm(both, high)
@@ -395,8 +403,8 @@
         row = (group * 8) % tile_rows
         for a in range(here):
             dest = a * per_row + (group * 8) // tile_rows
-            for c in range(FIELDS):
-                piece = result[8 * a : 8 * a + 8, RADIX * c : RADIX * (c + 1)]
+            for spot, c in enumerate(fields):
+                piece = result[8 * a : 8 * a + 8, RADIX * spot : RADIX * (spot + 1)]
                 if added:
                     piece = piece + sum_ref[dest, c, pl.ds(row, 8), :]
                 if special:
@@ -404,13 +412,13 @@
                     edge = edge_ref[c, pl.ds(a * RADIX + group * 8, 8), :]
                     edge = jnp.where(lane < HALF, edge[:, 0:1], edge[:, 1:2])
                     piece = jnp.where((lane % HALF == 0) & (flag_ref[0] == 0), edge, piece)
-                out_ref[dest, c, pl.ds(row, 8), :] = piece
+                out_ref[dest, spot, pl.ds(row, 8), :] = piece
         return carry
 
-    lax.fori_loop(0, RADIX // 8, second, 0)
-
-
-def column_inverse(part, start, wave_x, odd_x, place, edge, partial_sum, sizes):
+    lax.fori_loop(0, RADIX // 8, second, 0, unroll=8)
+
+
+def column_inverse(part, start, wave_x, odd_x, place, edge, partial_sum, sizes, fields):
     grid_len, wide_count, tile_rows = sizes
     flag, row_start, row_share = place
     piece, below, above = part
@@ -437,7 +445,7 @@
     operands = [*tables, *extra]
     plain = [pl.BlockSpec(memory_space=pltpu.VMEM)]
     square = (RADIX, RADIX)
-    out_shape = (wide_count, FIELDS, tile_rows, RADIX)
+    out_shape = (wide_count, len(fields), tile_rows, RADIX)
     return pl.pallas_call(
         functools.partial(
             column_inverse_kernel,
@@ -448,6 +456,7 @@
             int(edge is not None),
             int(partial_sum is not None),
             (tuple(below), tuple(above)),
+            fields,
         ),
         in_specs=[pl.BlockSpec(memory_space=pltpu.SMEM)]
         + plain * 2
@@ -456,15 +465,15 @@
         out_specs=pl.BlockSpec(memory_space=pltpu.VMEM),
         out_shape=jax.ShapeDtypeStruct(out_shape, jnp.float32),
         scratch_shapes=[
-            pltpu.VMEM((count * RADIX, FIELDS * RADIX), jnp.float32),
+            pltpu.VMEM((count * RADIX, len(fields) * RADIX), jnp.float32),
             pltpu.VMEM(square, jnp.float32),
             pltpu.VMEM(square, jnp.float32),
-            pltpu.VMEM((3, count * RADIX, RADIX), jnp.float32),
-            pltpu.SemaphoreType.DMA((3,)),
+            pltpu.VMEM((3 if below else 1, count * RADIX, RADIX), jnp.float32),
+            pltpu.SemaphoreType.DMA((3 if below else 1,)),
         ],
         compiler_params=pltpu.CompilerParams(vmem_limit_bytes=VMEM_LIMIT),
         cost_estimate=pl.CostEstimate(
-            flops=FIELDS * 45 * count * RADIX * RADIX * 256,
+            flops=len(fields) * 45 * count * RADIX * RADIX * 256,
             bytes_accessed=4 * (count * RADIX * RADIX + math.prod(out_shape)),
             transcendentals=count * RADIX * RADIX,
         ),
@@ -472,9 +481,11 @@
     )(flag, wave_x, odd_x, *moved, *operands)
 
 
-def row_inverse_kernel(chunks, *refs):
-    ins = refs[:chunks]
-    kh, kl, base, zero, cw, sw, out_ref, th, tl, rot, u_ref = refs[chunks:]
+def row_inverse_kernel(chunks, fields, *refs):
+    ins, refs = refs[: chunks * fields], refs[chunks * fields :]
+    kh, kl, base, zero, cw, sw = refs[:6]
+    trace_ref = refs[6] if len(refs) == 14 else None
+    out_ref, top_ref, bottom_ref, th, tl, rot, u_ref = refs[-7:]
     rows = ins[0].shape[2]
     outer_len = out_ref.shape[2] // RADIX
 
@@ -492,12 +503,16 @@
         parts = []
         for side in range(2):
             block = 2 * slot + side
-            item = ins[block % chunks][block // chunks]
-            parts.append(item.reshape(FIELDS * rows, RADIX))
+            parts.append(
+                jnp.concatenate(
+                    [ins[c * chunks + block % chunks][block // chunks, 0] for c in range(fields)],
+                    axis=0,
+                )
+            )
         u_ref[slot] = dot3(split(jnp.concatenate(parts, axis=1)), (th[slot], tl[slot]))
 
     table = (kh[...], kl[...])
-    for c in range(FIELDS):
+    for c in range(fields):
 
         def second(pair, carry):
             halves = []
@@ -521,54 +536,94 @@
                     ] = result[8 * a : 8 * a + 8, RADIX * side : RADIX * (side + 1)]
             return carry
 
-        lax.fori_loop(0, rows // 16, second, 0)
-    out_ref[FIELDS] = -(out_ref[0] + out_ref[3])
-
-
-def row_inverse(blocks, grid_len):
-    chunks = len(blocks)
-    wide_count, _, rows, _ = blocks[0].shape
-    step = min(rows, 32)
+        lax.fori_loop(0, rows // 16, second, 0, unroll=min(2, rows // 16))
+    if trace_ref is not None:
+        out_ref[fields] = -(trace_ref[0] + out_ref[0])
+    elif fields == FIELDS:
+        out_ref[fields] = -(out_ref[0] + out_ref[3])
+
+    @pl.when(pl.program_id(0) == 0)
+    def _():
+        top_ref[...] = out_ref[:, 0:8, :]
+
+    @pl.when(pl.program_id(0) == pl.num_programs(0) - 1)
+    def _():
+        bottom_ref[...] = out_ref[:, rows - 8 : rows, :]
+
+
+def row_inverse(pieces, grid_len, earlier):
+    fields, chunks = len(pieces), len(pieces[0])
+    wide_count, _, rows, _ = pieces[0][0][0].shape
+    step = min(rows, 32 if fields == FIELDS else 64)
+    made = FIELDS + 1 if fields == FIELDS else 3
     kron, base, zero, cw, sw = row_inverse_tables(grid_len)
     tables = (*np_split(kron), f32(base), f32(zero), f32(cw), f32(sw))
+    specs, operands = [], []
+    for per_chunk in pieces:
+        for array, index in per_chunk:
+            specs.append(
+                pl.BlockSpec((wide_count, 1, step, RADIX), lambda i, index=index: (0, index, i, 0))
+            )
+            operands.append(array)
+    specs += [full_spec(item.shape) for item in tables]
+    operands += tables
+    aliases = {}
+    if earlier is not None:
+        aliases = {len(operands): 0}
+        specs.append(pl.BlockSpec((1, step, grid_len), lambda i: (0, i, 0)))
+        operands.append(earlier)
+    group = 0 if earlier is None else 1
+    edge = jax.ShapeDtypeStruct((made, 8, grid_len), jnp.float32)
     return pl.pallas_call(
-        functools.partial(row_inverse_kernel, chunks),
+        functools.partial(row_inverse_kernel, chunks, fields),
         grid=(rows // step,),
-        in_specs=[pl.BlockSpec((wide_count, FIELDS, step, RADIX), lambda i: (0, 0, i, 0))] * chunks
-        + [full_spec(item.shape) for item in tables],
-        out_specs=pl.BlockSpec((FIELDS + 1, step, grid_len), lambda i: (0, i, 0)),
-        out_shape=jax.ShapeDtypeStruct((FIELDS + 1, rows, grid_len), jnp.float32),
+        in_specs=specs,
+        out_specs=[pl.BlockSpec((made, step, grid_len), lambda i: (group, i, 0))]
+        + [full_spec(edge.shape)] * 2,
+        out_shape=[jax.ShapeDtypeStruct((FIELDS + 1, rows, grid_len), jnp.float32), edge, edge],
         scratch_shapes=[
             pltpu.VMEM((SLOTS, 256, 256), jnp.bfloat16),
             pltpu.VMEM((SLOTS, 256, 256), jnp.bfloat16),
             pltpu.VMEM((256, 256), jnp.float32),
-            pltpu.VMEM((SLOTS, FIELDS * step, 256), jnp.float32),
+            pltpu.VMEM((SLOTS, fields * step, 256), jnp.float32),
         ],
+        input_output_aliases=aliases,
         compiler_params=pltpu.CompilerParams(vmem_limit_bytes=VMEM_LIMIT),
         cost_estimate=pl.CostEstimate(
-            flops=12 * FIELDS * rows * grid_len * 256,
-            bytes_accessed=44 * rows * grid_len,
+            flops=12 * fields * rows * grid_len * 256,
+            bytes_accessed=8 * fields * rows * grid_len,
             transcendentals=0,
         ),
         name="row_inverse",
-    )(*blocks, *tables)
-
-
-def interpolate_kernel(g_ref, halo_ref, wy_ref, col_ref, wx_ref, place_ref, out_ref, mask_ref):
+    )(*operands)
+
+
+def mask_kernel(col_ref, wx_ref, mask_ref):
+    samples, wide = mask_ref.shape
+    lane = pl.program_id(0) * wide + lax.broadcasted_iota(jnp.int32, (samples, wide), 1)
+    total = jnp.zeros((samples, wide), jnp.float32)
+    for tap in range(4):
+        here = lane == col_ref[:, tap : tap + 1]
+        total = total + jnp.where(here, wx_ref[:, tap : tap + 1], 0.0)
+    mask_ref[...] = total
+
+
+def column_mask(col_ids, weight_x, grid_len):
+    samples = col_ids.shape[0]
+    wide = 512
+    return pl.pallas_call(
+        mask_kernel,
+        grid=(grid_len // wide,),
+        in_specs=[full_spec(col_ids.shape), full_spec(weight_x.shape)],
+        out_specs=pl.BlockSpec((samples, wide), lambda i: (0, i)),
+        out_shape=jax.ShapeDtypeStruct((samples, grid_len), jnp.float32),
+        name="column_mask",
+    )(col_ids, weight_x)
+
+
+def interpolate_kernel(g_ref, halo_ref, wy_ref, mask_ref, place_ref, out_ref):
     samples, grid_len = mask_ref.shape
     wide = 512
-
-    @pl.when(pl.program_id(0) == 0)
-    def _():
-        for start in range(0, grid_len, wide):
-            lane = start + lax.broadcasted_iota(jnp.int32, (samples, wide), 1)
-            total = jnp.zeros((samples, wide), jnp.float32)
-            for tap in range(4):
-                total = total + jnp.where(
-                    lane == col_ref[:, tap : tap + 1], wx_ref[:, tap : tap + 1], 0.0
-                )
-            mask_ref[:, start : start + wide] = total
-
     left = split(wy_ref[...])
     partial = jnp.zeros((samples, RADIX), jnp.float32)
     for start in range(0, grid_len, wide):
@@ -581,21 +636,20 @@
     out_ref[0] = jnp.sum(value * place_ref[...], axis=0, keepdims=True)
 
 
-def interpolate(gradient, halo, weight_y, col_ids, weight_x, placement):
+def interpolate(gradient, halo, group, weight_y, mask, placement):
     _, rows, grid_len = gradient.shape
-    samples, slot_total = placement.shape
-    small = (weight_y, col_ids, weight_x, placement)
+    slot_total = placement.shape[1]
+    small = (weight_y, mask, placement)
     return pl.pallas_call(
         interpolate_kernel,
-        grid=(FIELDS,),
+        grid=(len(group),),
         in_specs=[
-            pl.BlockSpec((1, rows, grid_len), lambda i: (i, 0, 0)),
+            pl.BlockSpec((1, rows, grid_len), lambda i: (i + group[0], 0, 0)),
             pl.BlockSpec((1, 8, grid_len), lambda i: (i, 0, 0)),
         ]
         + [full_spec(item.shape) for item in small],
         out_specs=pl.BlockSpec((1, 1, slot_total), lambda i: (i, 0, 0)),
-        out_shape=jax.ShapeDtypeStruct((FIELDS, 1, slot_total), jnp.float32),
-        scratch_shapes=[pltpu.VMEM((samples, grid_len), jnp.float32)],
+        out_shape=jax.ShapeDtypeStruct((len(group), 1, slot_total), jnp.float32),
         compiler_params=pltpu.CompilerParams(vmem_limit_bytes=VMEM_LIMIT),
         name="interpolate",
     )(gradient, halo, *small)
@@ -696,7 +750,7 @@
     return picked
 
 
-def depth_scan(pieces, jobs, total, aside):
+def depth_scan(pieces, jobs, total):
     count = lax.axis_size("depth")
     here = lax.axis_index("depth")
     up = [(i, i + 1) for i in range(count - 1)]
@@ -714,14 +768,16 @@
         falling = choose(here, {count - 1 - d: pieces[step - d] for d in live})
         if step:
             rising, falling = rising + from_below[-1], falling + from_above[-1]
-        work = [jobs[step]] if step in jobs else []
-        if step == aside[0]:
-            work.append(aside[1:])
+        work = jobs.get(step, [])
         keys = [key for _, key in work]
         rising, falling, keys = lax.optimization_barrier((rising, falling, keys))
         below = lax.ppermute(rising, "depth", up)
         above = lax.ppermute(falling, "depth", down)
-        results = [task(key, complete) for (task, _), key in zip(work, keys)]
+        results = []
+        for (task, _), key in zip(work, keys):
+            if results:
+                key, _ = lax.optimization_barrier((key, results[-1]))
+            results.append(task(key, complete))
         below, above, _ = lax.optimization_barrier((below, above, results))
         from_below.append(below)
         from_above.append(above)
@@ -740,7 +796,12 @@
     def exchange(block):
         return lax.all_to_all(block, "wide", split_axis=0, concat_axis=0, tiled=True)
 
-    spectra = [exchange(item) for item in row_forward(density[0], wide_count)]
+    groups = [range(0, SLOTS, 2), range(1, SLOTS, 2)] if chunks == 4 else [range(SLOTS)]
+    spectra, field = [], density[0]
+    for group in groups:
+        made = row_forward(field, wide_count, tuple(group))
+        spectra += [exchange(item) for item in made]
+        field, _ = lax.optimization_barrier((field, made[0]))
     columns = [item.reshape(grid_len, RADIX) for item in spectra]
 
     lane = jnp.arange(RADIX, dtype=jnp.int32)[None, :] % HALF
@@ -765,51 +826,6 @@
     row_start = depth_id * row_share
     place = (jnp.stack([wide_id, depth_id]).astype(jnp.int32), row_start, row_share)
     sizes = (grid_len, wide_count, tile_rows)
-    pieces, blocks, partial_sums, edges = [], {}, {}, []
-
-    def forward_job(chunk, wave, complete):
-        pieces.extend(column_forward(columns[chunk], wave, depths))
-        return pieces[-1]
-
-    def edge_job(key, complete):
-        edges.append(edge_inverse(key, row_start, row_share))
-        return edges[0]
-
-    def early_job(chunk, wave, complete):
-        item = column_inverse(complete(2 * chunk), 0, wave, wave, place, None, None, sizes)
-        partial_sums[chunk] = item
-        return item
-
-    def late_job(chunk, wave, complete):
-        part = complete(2 * chunk + 1)
-        special = edges[0] if chunk == 0 else None
-        item = column_inverse(
-            part, outer_len // 2, wave, wave, place, special, partial_sums[chunk], sizes
-        )
-        blocks[chunk] = exchange(item)
-        return item
-
-    forward_job(0, waves[0], None)
-    jobs = {}
-    last = chunks - 1
-    for chunk in range(chunks):
-        if chunk:
-            jobs[chunk - 1] = (functools.partial(forward_job, chunk), waves[chunk])
-        jobs[2 * chunk + depth_count - 1] = (functools.partial(early_job, chunk), waves[chunk])
-        if chunk < last:
-            jobs[2 * chunk + depth_count] = (functools.partial(late_job, chunk), waves[chunk])
-    complete = depth_scan(pieces, jobs, 2 * chunks, (EDGE_STEP, edge_job, edge))
-    late_job(last, waves[last], complete)
-    blocks = [blocks[chunk] for chunk in range(chunks)]
-    gradient = row_inverse(blocks, grid_len)
-
-    tiles = depth_count * wide_count
-    forward = [(i, (i + 1) % tiles) for i in range(tiles)]
-    backward = [(target, source) for source, target in forward]
-    low = lax.ppermute(gradient[:FIELDS, tile_rows - 2 :], ("depth", "wide"), forward)
-    high = lax.ppermute(gradient[:FIELDS, :2], ("depth", "wide"), backward)
-    halo = jnp.concatenate([low, high, jnp.zeros((FIELDS, 4, grid_len), jnp.float32)], axis=1)
-
     taps_y, offset_y = tap_weights(sample_frac[0, 0])
     taps_x, offset_x = tap_weights(sample_frac[0, 1])
     row_ids = sample_row[0][:, None] + offset_y
@@ -832,7 +848,75 @@
     placement = (target[:, None] == jnp.arange(slot_total, dtype=jnp.int32)[None, :]).astype(
         jnp.float32
     )
-    outgoing = interpolate(gradient, halo, weight_y, col_ids, taps_x, placement)
+    pieces, blocks, partial_sums, edges = [], {}, {}, []
+
+    def forward_job(chunk, wave, complete):
+        pieces.extend(column_forward(columns[chunk], wave, depths))
+        return pieces[-1]
+
+    def edge_job(key, complete):
+        edges.append(edge_inverse(key[0], row_start, row_share))
+        edges.append(column_mask(key[1], taps_x, grid_len))
+        return edges
+
+    def early_job(chunk, wave, complete):
+        item = column_inverse(complete(2 * chunk), 0, wave, wave, place, None, None, sizes, EVERY)
+        partial_sums[chunk] = item
+        return item
+
+    def late_job(chunk, wave, complete, groups=(EVERY,)):
+        part = complete(2 * chunk + 1)
+        special = edges[0] if chunk == 0 else None
+        for group in groups:
+            item = column_inverse(
+                part, outer_len // 2, wave, wave, place, special, partial_sums[chunk], sizes, group
+            )
+            moved = exchange(item)
+            for spot, c in enumerate(group):
+                blocks[c, chunk] = (moved, spot)
+            if group != groups[-1]:
+                wave, _ = lax.optimization_barrier((wave, item))
+        return item
+
+    forward_job(0, waves[0], None)
+    jobs = {}
+    last = chunks - 1
+
+    def plan(step, task, chunk):
+        jobs.setdefault(step, []).append((functools.partial(task, chunk), waves[chunk]))
+
+    for chunk in range(1, chunks):
+        plan(chunk - 1, forward_job, chunk)
+    for chunk in range(chunks):
+        plan(2 * chunk + depth_count - 1, early_job, chunk)
+        if chunk != last:
+            plan(2 * chunk + depth_count, late_job, chunk)
+    jobs.setdefault(EDGE_STEP, []).append((edge_job, (edge, col_ids)))
+    complete = depth_scan(pieces, jobs, 2 * chunks)
+    late_job(last, waves[last], complete, GROUPS)
+
+    tiles = depth_count * wide_count
+    forward = [(i, (i + 1) % tiles) for i in range(tiles)]
+    backward = [(target, source) for source, target in forward]
+    gradient, halos = None, []
+    for group in GROUPS:
+        ready = [[blocks[c, chunk] for chunk in range(chunks)] for c in group]
+        gradient, top, bottom = row_inverse(ready, grid_len, gradient)
+        used = len(group)
+        gradient, bottom, top = lax.optimization_barrier(
+            (gradient, bottom[:used, 6:], top[:used, :2])
+        )
+        low = lax.ppermute(bottom, ("depth", "wide"), forward)
+        high = lax.ppermute(top, ("depth", "wide"), backward)
+        halos.append(
+            jnp.concatenate([low, high, jnp.zeros((used, 4, grid_len), jnp.float32)], axis=1)
+        )
+
+    outgoing = [
+        interpolate(gradient, halo, group, weight_y, edges[1], placement)
+        for group, halo in zip(GROUPS, halos)
+    ]
+    outgoing = jnp.concatenate(outgoing)
     outgoing = outgoing.reshape(FIELDS, wide_count, capacity)
     arrived = lax.all_to_all(outgoing, "wide", split_axis=1, concat_axis=1, tiled=True)
     arrived = arrived.reshape(FIELDS, 1, slot_total)

time: 518 us -> 525 us (1.014); the launches traced: 516 us -> 515 us
  Pallas kernels: 235 us -> 188 us
  waiting for transfers between devices: 124 us -> 155 us
  other arithmetic: 25.1 us -> 33.6 us
  starting transfers between devices: 86.5 us -> 93.1 us
    pallas_call x8, Pallas kernels: 134 us -> 95.3 us  [column_inverse(): pl.pallas_call(functools.partial(column_inverse_kernel, grid_len, tile_ro...]
    ppermute x10, waiting for transfers between devices: 27.9 us -> 55.2 us  [depth_scan(): below = lax.ppermute(rising, 'depth', up)]
    pallas_call x4, Pallas kernels: 48.1 us -> 36.1 us  [column_forward(): pl.pallas_call(functools.partial(column_forward_kernel, grid_len), in_spe...]
    add x9, other arithmetic: 16.2 us -> 24 us  [depth_scan(): rising, falling = (rising + from_below[-1], falling + from_above[-1])]
    pallas_call x3 -> x5, Pallas kernels: 52.5 us -> 56.3 us  [the longest x2 21.4 us: row_forward(): pl.pallas_call(functools.partial(row_forward_kernel, chunks, slots), grid...]
  transfers between devices with their start and end apart: 31 -> 31, of which waited for: 22 -> 22; matrix products, arithmetic and copies ran while one was open for 7% -> 8% of each run, Pallas kernels for 35% -> 27%
where the time goes in v3:
time: 525 us; the launch traced here: 515 us
  Pallas kernels  188 us (36%)
  waiting for transfers between devices  155 us (30%)
  starting transfers between devices  93.1 us (18%)
  other arithmetic  33.6 us (6%)
  local copies, waits for them, and re-layouts  18.1 us (3%)
  between operations  16.6 us (3%)
  blocking collectives  7.5 us (1%)
    pallas_call x8, Pallas kernels, column_inverse(): pl.pallas_call(functools.partial(column_inverse_kernel, grid_len, tile_ro...  95.3 us
    all_to_all x8, waiting for transfers between devices, exchange(): lax.all_to_all(block, 'wide', split_axis=0, concat_axis=0, tiled=True)  62.4 us
    ppermute x10, waiting for transfers between devices, depth_scan(): below = lax.ppermute(rising, 'depth', up)  55.2 us
    all_to_all x8, starting transfers between devices, exchange(): lax.all_to_all(block, 'wide', split_axis=0, concat_axis=0, tiled=True)  40 us
    pallas_call x4, Pallas kernels, column_forward(): pl.pallas_call(functools.partial(column_forward_kernel, grid_len), in_spe...  36.1 us
    ppermute x10, waiting for transfers between devices, depth_scan(): above = lax.ppermute(falling, 'depth', down)  34.9 us
    ppermute x10, starting transfers between devices, depth_scan(): below = lax.ppermute(rising, 'depth', up)  34.4 us
    add x9, other arithmetic, depth_scan(): rising, falling = (rising + from_below[-1], falling + from_above[-1])  24 us
  transfers between devices with their start and end apart: 31, of which 22 were waited for; matrix products, arithmetic and copies ran while one was open for 8% of the time, Pallas kernels for 27%

profile of v3, /device:TPU:0, one launch (start us, length us, event | category | flops | bytes accessed | tf_op | source)
XLA Modules:
  0.0 515.2 jit_solution(8796719577438005206)
XLA Ops:
  7.2 10.5 %row_forward.2 = (f32[8,512,128]{2,1,0:T(8,128)}, f32[8,512,128]{2,1,0:T(8,128)}) custom-call(f32[512,4096]{1,0:T(8,128)} %bitcast.91, bf16[128,256]{1,0:T(8,128)(2,1)} %constant.248.clone.kh, bf16[128,256]{1,0:T(8,128)(2,1)} %constant.249.clone.kl, f32[256,256]{1,0:T(8,128)} %constant.250.clone.base, f32[256,256]{1,0:T(8,128)} %constant.251.clone.zero, ...), custom_call_target="tpu_custom_call" | custom-call | flops 5368709120 | bytes 16777216 | tf_op jit(solution)/shard_map/row_forward/pallas_call | solution.py:199
  32.3 11.0 %row_forward.3 = (f32[8,512,128]{2,1,0:T(8,128)}, f32[8,512,128]{2,1,0:T(8,128)}) custom-call(f32[512,4096]{1,0:T(8,128)} %bitcast.92, bf16[128,256]{1,0:T(8,128)(2,1)} %constant.254.clone.kh, bf16[128,256]{1,0:T(8,128)(2,1)} %constant.255.clone.kl, f32[256,256]{1,0:T(8,128)} %constant.256.clone.base.zero, f32[256,256]{1,0:T(8,128)} %constant.256.clone.base.zero, ...), custom_call_target="tpu_custom_call" | custom-call | flops 5368709120 | bytes 16777216 | tf_op jit(solution)/shard_map/row_forward/pallas_call | solution.py:199
  54.0 9.0 %column_forward.4 = (f32[2048,128]{1,0:T(8,128)}, f32[2048,128]{1,0:T(8,128)}) custom-call(f32[2]{0:T(128)} %pad_maximum_fusion.5.depth_ref, f32[4096,128]{1,0:T(8,128)} %bitcast.73, f32[1,128]{1,0:T(1,128)} %convert_multiply_fusion.3.kx_ref.kxo_ref, bf16[256,512]{1,0:T(8,128)(2,1)} %constant.264.clone.kh, bf16[256,512]{1,0:T(8,128)(2,1)} %constant.265.clone.kl, ...), custom_call_target="tpu_custom_call" | custom-call | flops 13421772800 | bytes 4194304 | tf_op jit(solution)/shard_map/column_forward/pallas_call | solution.py:296
  85.0 9.1 %column_forward.5 = (f32[2048,128]{1,0:T(8,128)}, f32[2048,128]{1,0:T(8,128)}) custom-call(f32[2]{0:T(128)} %pad_maximum_fusion.5.depth_ref, f32[4096,128]{1,0:T(8,128)} %bitcast.3.x_ref, f32[1,128]{1,0:T(1,128)} %get-tuple-element.122.kx_ref.kxo_ref, bf16[256,512]{1,0:T(8,128)(2,1)} %constant.264.clone.kh, bf16[256,512]{1,0:T(8,128)(2,1)} %constant.265.clone.kl, ...), custom_call_target="tpu_custom_call" | custom-call | flops 13421772800 | bytes 4194304 | tf_op jit(solution)/shard_map/column_forward/pallas_call | solution.py:296
  103.5 8.1 %all-to-all-done.2 = f32[8,512,128]{2,1,0:T(8,128)} async-done(((f32[8,512,128]{2,1,0:T(8,128)}), f32[8,512,128]{2,1,0:T(8,128)}, u32[]{:S(2)}, u32[]{:S(2)}) %all-to-all-start.2) | async-done | bytes 2097184 | tf_op jit(solution)/shard_map/all_to_all | solution.py:797
  116.5 9.1 %column_forward.6 = (f32[2048,128]{1,0:T(8,128)}, f32[2048,128]{1,0:T(8,128)}) custom-call(f32[2]{0:T(128)} %pad_maximum_fusion.5.depth_ref, f32[4096,128]{1,0:T(8,128)} %bitcast.5.x_ref, f32[1,128]{1,0:T(1,128)} %get-tuple-element.132.kx_ref.kxo_ref, bf16[256,512]{1,0:T(8,128)(2,1)} %constant.264.clone.kh, bf16[256,512]{1,0:T(8,128)(2,1)} %constant.265.clone.kl, ...), custom_call_target="tpu_custom_call" | custom-call | flops 13421772800 | bytes 4194304 | tf_op jit(solution)/shard_map/column_forward/pallas_call | solution.py:296
  132.7 10.4 %all-to-all-done.3 = f32[8,512,128]{2,1,0:T(8,128)} async-done(((f32[8,512,128]{2,1,0:T(8,128)}), f32[8,512,128]{2,1,0:T(8,128)}, u32[]{:S(2)}, u32[]{:S(2)}) %all-to-all-start.3) | async-done | bytes 2097184 | tf_op jit(solution)/shard_map/all_to_all | solution.py:797
  143.1 9.0 %column_forward.7 = (f32[2048,128]{1,0:T(8,128)}, f32[2048,128]{1,0:T(8,128)}) custom-call(f32[2]{0:T(128)} %pad_maximum_fusion.5.depth_ref, f32[4096,128]{1,0:T(8,128)} %bitcast.18.x_ref, f32[1,128]{1,0:T(1,128)} %convert_multiply_fusion.kx_ref.kxo_ref, bf16[256,512]{1,0:T(8,128)(2,1)} %constant.264.clone.kh, bf16[256,512]{1,0:T(8,128)(2,1)} %constant.265.clone.kl, ...), custom_call_target="tpu_custom_call" | custom-call | flops 13421772800 | bytes 4194304 | tf_op jit(solution)/shard_map/column_forward/pallas_call | solution.py:296
  187.2 11.1 %column_inverse.8.refs_14_ = f32[8,5,128,128]{3,2,1,0:T(8,128)} custom-call(s32[2]{0:T(128)} %pad_add_fusion.flag_ref, f32[1,128]{1,0:T(1,128)} %convert_multiply_fusion.3.kx_ref.kxo_ref, f32[1,128]{1,0:T(1,128)} %convert_multiply_fusion.3.kx_ref.kxo_ref, f32[2048,128]{1,0:T(8,128)} %get-tuple-element.85.refs_0_, f32[2048,128]{1,0:T(8,128)} %copy-done.17, ...), custom_call_target="tpu_custom_call" | custom-call | flops 15099494400 | bytes 3670016 | tf_op jit(solution)/shard_map/column_inverse/pallas_call | solution.py:449
  215.7 14.5 %column_inverse.9 = f32[8,5,128,128]{3,2,1,0:T(8,128)} custom-call(s32[2]{0:T(128)} %pad_add_fusion.flag_ref, f32[1,128]{1,0:T(1,128)} %convert_multiply_fusion.3.kx_ref.kxo_ref, f32[1,128]{1,0:T(1,128)} %convert_multiply_fusion.3.kx_ref.kxo_ref, f32[2048,128]{1,0:T(8,128)} %get-tuple-element.83.refs_0_, f32[2048,128]{1,0:T(8,128)} %collective-permute-done.2.refs_2_.refs_1_, ...), custom_call_target="tpu_custom_call" | custom-call | flops 15099494400 | bytes 3670016 | tf_op jit(solution)/shard_map/column_inverse/pallas_call | solution.py:449
  230.3 8.2 %all-to-all-start.4 = ((f32[8,5,128,128]{3,2,1,0:T(8,128)}), f32[8,5,128,128]{3,2,1,0:T(8,128)S(1)}, u32[]{:S(2)}, u32[]{:S(2)}) async-start(f32[8,5,128,128]{3,2,1,0:T(8,128)} %column_inverse.9), calls=%async_computation.4 | async-start | bytes 5242880 | tf_op jit(solution)/shard_map/all_to_all | solution.py:797
  248.8 11.0 %column_inverse.10.refs_13_ = f32[8,5,128,128]{3,2,1,0:T(8,128)} custom-call(s32[2]{0:T(128)} %pad_add_fusion.flag_ref, f32[1,128]{1,0:T(1,128)} %get-tuple-element.122.kx_ref.kxo_ref, f32[1,128]{1,0:T(1,128)} %get-tuple-element.122.kx_ref.kxo_ref, f32[2048,128]{1,0:T(8,128)} %get-tuple-element.79.refs_0_, ...), custom_call_target="tpu_custom_call" | custom-call | flops 15099494400 | bytes 3670016 | tf_op jit(solution)/shard_map/column_inverse/pallas_call | solution.py:449
  259.9 11.0 %collective-permute-done.10.refs_3_.refs_2_.refs_1_ = f32[2048,128]{1,0:T(8,128)S(1)} collective-permute-done((f32[2048,128]{1,0:T(8,128)}, f32[2048,128]{1,0:T(8,128)S(1)}, u32[]{:S(2)}, u32[]{:S(2)}) %collective-permute-start.10) | collective-permute-done | bytes 1048608 | tf_op jit(solution)/shard_map/ppermute | solution.py:774
  281.4 12.2 %column_inverse.11 = f32[8,5,128,128]{3,2,1,0:T(8,128)} custom-call(s32[2]{0:T(128)} %pad_add_fusion.flag_ref, f32[1,128]{1,0:T(1,128)} %get-tuple-element.122.kx_ref.kxo_ref, f32[1,128]{1,0:T(1,128)} %get-tuple-element.122.kx_ref.kxo_ref, f32[2048,128]{1,0:T(8,128)} %get-tuple-element.80.refs_0_, f32[2048,128]{1,0:T(8,128)} %copy-done.21, ...), custom_call_target="tpu_custom_call" | custom-call | flops 15099494400 | bytes 3670016 | tf_op jit(solution)/shard_map/column_inverse/pallas_call | solution.py:449
  293.7 9.0 %collective-permute-done.12.refs_3_.refs_2_.refs_1_ = f32[2048,128]{1,0:T(8,128)S(1)} collective-permute-done((f32[2048,128]{1,0:T(8,128)}, f32[2048,128]{1,0:T(8,128)S(1)}, u32[]{:S(2)}, u32[]{:S(2)}) %collective-permute-start.12) | collective-permute-done | bytes 1048608 | tf_op jit(solution)/shard_map/ppermute | solution.py:774
  313.4 11.0 %column_inverse.12.refs_13_ = f32[8,5,128,128]{3,2,1,0:T(8,128)} custom-call(s32[2]{0:T(128)} %pad_add_fusion.flag_ref, f32[1,128]{1,0:T(1,128)} %get-tuple-element.132.kx_ref.kxo_ref, f32[1,128]{1,0:T(1,128)} %get-tuple-element.132.kx_ref.kxo_ref, f32[2048,128]{1,0:T(8,128)} %get-tuple-element.89.refs_0_, ...), custom_call_target="tpu_custom_call" | custom-call | flops 15099494400 | bytes 3670016 | tf_op jit(solution)/shard_map/column_inverse/pallas_call | solution.py:449
  324.4 9.1 %collective-permute-done.14.refs_3_.refs_2_.refs_1_ = f32[2048,128]{1,0:T(8,128)S(1)} collective-permute-done((f32[2048,128]{1,0:T(8,128)}, f32[2048,128]{1,0:T(8,128)S(1)}, u32[]{:S(2)}, u32[]{:S(2)}) %collective-permute-start.14) | collective-permute-done | bytes 1048608 | tf_op jit(solution)/shard_map/ppermute | solution.py:774
  349.8 12.2 %column_inverse.13 = f32[8,5,128,128]{3,2,1,0:T(8,128)} custom-call(s32[2]{0:T(128)} %pad_add_fusion.flag_ref, f32[1,128]{1,0:T(1,128)} %get-tuple-element.132.kx_ref.kxo_ref, f32[1,128]{1,0:T(1,128)} %get-tuple-element.132.kx_ref.kxo_ref, f32[2048,128]{1,0:T(8,128)} %get-tuple-element.92.refs_0_, f32[2048,128]{1,0:T(8,128)} %copy-done.20, ...), custom_call_target="tpu_custom_call" | custom-call | flops 15099494400 | bytes 3670016 | tf_op jit(solution)/shard_map/column_inverse/pallas_call | solution.py:449
  362.0 9.3 %collective-permute-done.16.refs_3_.refs_2_ = f32[2048,128]{1,0:T(8,128)S(1)} collective-permute-done((f32[2048,128]{1,0:T(8,128)S(1)}, f32[2048,128]{1,0:T(8,128)S(1)}, u32[]{:S(2)}, u32[]{:S(2)}) %collective-permute-start.16) | collective-permute-done | bytes 1048608 | tf_op jit(solution)/shard_map/ppermute | solution.py:774
  385.8 11.0 %column_inverse.14.refs_13_ = f32[8,5,128,128]{3,2,1,0:T(8,128)} custom-call(s32[2]{0:T(128)} %pad_add_fusion.flag_ref, f32[1,128]{1,0:T(1,128)} %convert_multiply_fusion.kx_ref.kxo_ref, f32[1,128]{1,0:T(1,128)} %convert_multiply_fusion.kx_ref.kxo_ref, f32[2048,128]{1,0:T(8,128)} %get-tuple-element.112.refs_0_, f32[2048,128]{1,0:T(8,128)} %copy-done.18, ...), custom_call_target="tpu_custom_call" | custom-call | flops 15099494400 | bytes 3670016 | tf_op jit(solution)/shard_map/column_inverse/pallas_call | solution.py:449
  406.9 12.2 %column_inverse.15 = f32[8,5,128,128]{3,2,1,0:T(8,128)} custom-call(s32[2]{0:T(128)} %pad_add_fusion.flag_ref, f32[1,128]{1,0:T(1,128)} %convert_multiply_fusion.kx_ref.kxo_ref, f32[1,128]{1,0:T(1,128)} %convert_multiply_fusion.kx_ref.kxo_ref, f32[2048,128]{1,0:T(8,128)} %get-tuple-element.99.refs_0_, f32[2048,128]{1,0:T(8,128)} %copy-done.19, ...), custom_call_target="tpu_custom_call" | custom-call | flops 15099494400 | bytes 3670016 | tf_op jit(solution)/shard_map/column_inverse/pallas_call | solution.py:449
  426.6 30.8 %all-to-all-done.7.refs_3_.refs_7_.refs_11_.refs_15_.refs_19_ = f32[8,5,128,128]{3,2,1,0:T(8,128)} async-done(((f32[8,5,128,128]{3,2,1,0:T(8,128)}), f32[8,5,128,128]{3,2,1,0:T(8,128)}, u32[]{:S(2)}, u32[]{:S(2)}) %all-to-all-start.7) | async-done | bytes 2621472 | tf_op jit(solution)/shard_map/all_to_all | solution.py:797
  457.3 15.3 %row_inverse.1 = (f32[6,128,4096]{2,1,0:T(8,128)}, f32[6,8,4096]{2,1,0:T(8,128)}, f32[6,8,4096]{2,1,0:T(8,128)}) custom-call(f32[8,5,128,128]{3,2,1,0:T(8,128)} %copy-done, f32[8,5,128,128]{3,2,1,0:T(8,128)} %all-to-all-done.5.refs_1_.refs_5_.refs_9_.refs_13_.refs_17_, f32[8,5,128,128]{3,2,1,0:T(8,128)} %copy-done.1, ...), custom_call_target="tpu_custom_call" | custom-call | flops 8053063680 | bytes 20971520 | tf_op jit(solution)/shard_map/row_inverse/pallas_call | solution.py:577
  484.4 13.0 %interpolate.1 = f32[5,1,512]{2,1,0:T(1,128)} custom-call(f32[6,128,4096]{2,1,0:T(8,128)} %get-tuple-element.152.g_ref, f32[5,8,4096]{2,1,0:T(8,128)} %maximum_maximum_fusion.halo_ref, f32[256,136]{1,0:T(8,128)} %copy.134.wy_ref, f32[256,4096]{1,0:T(8,128)} %column_mask.1.mask_ref, f32[256,512]{1,0:T(8,128)} %fusion.5.place_ref), custom_call_target="tpu_custom_call" | custom-call | tf_op jit(solution)/shard_map/interpolate/pallas_call | solution.py:643
  (200 shorter events, 221.6 us)
Async XLA Ops:
  17.6 32.0 %all-to-all-start.1 = ((f32[8,512,128]{2,1,0:T(8,128)}), f32[8,512,128]{2,1,0:T(8,128)S(1)}, u32[]{:S(2)}, u32[]{:S(2)}) async-start(f32[8,512,128]{2,1,0:T(8,128)} %get-tuple-element.76), calls=%async_computation.1 | async-start | bytes 4194304 | tf_op jit(solution)/shard_map/all_to_all | solution.py:797
  49.6 31.0 %all-to-all-start = ((f32[8,512,128]{2,1,0:T(8,128)}), f32[8,512,128]{2,1,0:T(8,128)}, u32[]{:S(2)}, u32[]{:S(2)}) async-start(f32[8,512,128]{2,1,0:T(8,128)} %get-tuple-element.75), calls=%async_computation | async-start | bytes 4194304 | tf_op jit(solution)/shard_map/all_to_all | solution.py:797
  54.0 78.8 %all-reduce.2.cloned.1.call-start = ((), (), s32[]{:S(2)}) async-start(), calls=%async_computation.9 | async-start | bytes 131072 | tf_op jit(solution)/shard_map/psum | solution.py:824
  63.1 31.0 %collective-permute-start = (f32[2048,128]{1,0:T(8,128)}, f32[2048,128]{1,0:T(8,128)S(1)}, u32[]{:S(2)}, u32[]{:S(2)}) collective-permute-start(f32[2048,128]{1,0:T(8,128)} %get-tuple-element.85.refs_0_), channel_id=1, source_target_pairs={{0,8},{8,16},{16,24},{1,9},{9,17},{17,25},{2,10},{10,18},{18,26},{... | collective-permute-start | bytes 3145736 | tf_op jit(solution)/shard_map/ppermute | solution.py:774
  66.7 28.4 %collective-permute-start.1 = (f32[2048,128]{1,0:T(8,128)}, f32[2048,128]{1,0:T(8,128)}, u32[]{:S(2)}, u32[]{:S(2)}) collective-permute-start(f32[2048,128]{1,0:T(8,128)} %get-tuple-element.85.refs_0_), channel_id=1, source_target_pairs={{8,0},{16,8},{24,16},{9,1},{17,9},{25,17},{10,2},{18,10},{26,18},{... | collective-permute-start | bytes 3145736 | tf_op jit(solution)/shard_map/ppermute | solution.py:775
  80.6 31.0 %all-to-all-start.2 = ((f32[8,512,128]{2,1,0:T(8,128)}), f32[8,512,128]{2,1,0:T(8,128)}, u32[]{:S(2)}, u32[]{:S(2)}) async-start(f32[8,512,128]{2,1,0:T(8,128)} %get-tuple-element.82), calls=%async_computation.2 | async-start | bytes 4194304 | tf_op jit(solution)/shard_map/all_to_all | solution.py:797
  97.8 27.7 %collective-permute-start.2 = (f32[2048,128]{1,0:T(8,128)}, f32[2048,128]{1,0:T(8,128)}, u32[]{:S(2)}, u32[]{:S(2)}) collective-permute-start(f32[2048,128]{1,0:T(8,128)} %get-tuple-element.90), channel_id=1, source_target_pairs={{0,8},{8,16},{16,24},{1,9},{9,17},{17,25},{2,10},{10,18},{18,26},{... | collective-permute-start | bytes 3145736 | tf_op jit(solution)/shard_map/ppermute | solution.py:774
  102.3 27.4 %collective-permute-start.3 = (f32[2048,128]{1,0:T(8,128)}, f32[2048,128]{1,0:T(8,128)}, u32[]{:S(2)}, u32[]{:S(2)}) collective-permute-start(f32[2048,128]{1,0:T(8,128)} %get-tuple-element.91), channel_id=1, source_target_pairs={{8,0},{16,8},{24,16},{9,1},{17,9},{25,17},{10,2},{18,10},{26,18},{... | collective-permute-start | bytes 3145736 | tf_op jit(solution)/shard_map/ppermute | solution.py:775
  111.6 31.5 %all-to-all-start.3 = ((f32[8,512,128]{2,1,0:T(8,128)}), f32[8,512,128]{2,1,0:T(8,128)}, u32[]{:S(2)}, u32[]{:S(2)}) async-start(f32[8,512,128]{2,1,0:T(8,128)} %get-tuple-element.97), calls=%async_computation.3 | async-start | bytes 4194304 | tf_op jit(solution)/shard_map/all_to_all | solution.py:797
  209.9 28.6 %collective-permute-start.8 = (f32[2048,128]{1,0:T(8,128)}, f32[2048,128]{1,0:T(8,128)}, u32[]{:S(2)}, u32[]{:S(2)}) collective-permute-start(f32[2048,128]{1,0:T(8,128)} %get-tuple-element.113), channel_id=1, source_target_pairs={{0,8},{8,16},{16,24},{1,9},{9,17},{17,25},{2,10},{10,18},{18,26},{... | collective-permute-start | bytes 3145736 | tf_op jit(solution)/shard_map/ppermute | solution.py:774
  214.3 24.2 %collective-permute-start.9 = (f32[2048,128]{1,0:T(8,128)}, f32[2048,128]{1,0:T(8,128)}, u32[]{:S(2)}, u32[]{:S(2)}) collective-permute-start(f32[2048,128]{1,0:T(8,128)} %get-tuple-element.114), channel_id=1, source_target_pairs={{8,0},{16,8},{24,16},{9,1},{17,9},{25,17},{10,2},{18,10},{26,18},{... | collective-permute-start | bytes 3145736 | tf_op jit(solution)/shard_map/ppermute | solution.py:775
  230.3 107.4 %all-to-all-start.4 = ((f32[8,5,128,128]{3,2,1,0:T(8,128)}), f32[8,5,128,128]{3,2,1,0:T(8,128)S(1)}, u32[]{:S(2)}, u32[]{:S(2)}) async-start(f32[8,5,128,128]{3,2,1,0:T(8,128)} %column_inverse.9), calls=%async_computation.4 | async-start | bytes 5242880 | tf_op jit(solution)/shard_map/all_to_all | solution.py:797
  242.7 28.2 %collective-permute-start.10 = (f32[2048,128]{1,0:T(8,128)}, f32[2048,128]{1,0:T(8,128)S(1)}, u32[]{:S(2)}, u32[]{:S(2)}) collective-permute-start(f32[2048,128]{1,0:T(8,128)} %get-tuple-element.117), channel_id=1, source_target_pairs={{0,8},{8,16},{16,24},{1,9},{9,17},{17,25},{2,10},{10,18},{18,26},{... | collective-permute-start | bytes 3145736 | tf_op jit(solution)/shard_map/ppermute | solution.py:774
  247.5 27.5 %collective-permute-start.11 = (f32[2048,128]{1,0:T(8,128)}, f32[2048,128]{1,0:T(8,128)}, u32[]{:S(2)}, u32[]{:S(2)}) collective-permute-start(f32[2048,128]{1,0:T(8,128)} %get-tuple-element.118), channel_id=1, source_target_pairs={{8,0},{16,8},{24,16},{9,1},{17,9},{25,17},{10,2},{18,10},{26,18},{... | collective-permute-start | bytes 3145736 | tf_op jit(solution)/shard_map/ppermute | solution.py:775
  277.8 24.9 %collective-permute-start.12 = (f32[2048,128]{1,0:T(8,128)}, f32[2048,128]{1,0:T(8,128)S(1)}, u32[]{:S(2)}, u32[]{:S(2)}) collective-permute-start(f32[2048,128]{1,0:T(8,128)} %get-tuple-element.123), channel_id=1, source_target_pairs={{0,8},{8,16},{16,24},{1,9},{9,17},{17,25},{2,10},{10,18},{18,26},{... | collective-permute-start | bytes 3145736 | tf_op jit(solution)/shard_map/ppermute | solution.py:774
  280.1 26.7 %collective-permute-start.13 = (f32[2048,128]{1,0:T(8,128)}, f32[2048,128]{1,0:T(8,128)}, u32[]{:S(2)}, u32[]{:S(2)}) collective-permute-start(f32[2048,128]{1,0:T(8,128)} %get-tuple-element.124), channel_id=1, source_target_pairs={{8,0},{16,8},{24,16},{9,1},{17,9},{25,17},{10,2},{18,10},{26,18},{... | collective-permute-start | bytes 3145736 | tf_op jit(solution)/shard_map/ppermute | solution.py:775
  311.9 25.8 %collective-permute-start.15 = (f32[2048,128]{1,0:T(8,128)}, f32[2048,128]{1,0:T(8,128)}, u32[]{:S(2)}, u32[]{:S(2)}) collective-permute-start(f32[2048,128]{1,0:T(8,128)} %get-tuple-element.128), channel_id=1, source_target_pairs={{8,0},{16,8},{24,16},{9,1},{17,9},{25,17},{10,2},{18,10},{26,18},{... | collective-permute-start | bytes 3145736 | tf_op jit(solution)/shard_map/ppermute | solution.py:775
  339.3 42.3 %all-to-all-start.5 = ((f32[8,5,128,128]{3,2,1,0:T(8,128)}), f32[8,5,128,128]{3,2,1,0:T(8,128)}, u32[]{:S(2)}, u32[]{:S(2)}) async-start(f32[8,5,128,128]{3,2,1,0:T(8,128)} %column_inverse.11), calls=%async_computation.5 | async-start | bytes 5242880 | tf_op jit(solution)/shard_map/all_to_all | solution.py:797
  346.1 25.2 %collective-permute-start.16 = (f32[2048,128]{1,0:T(8,128)S(1)}, f32[2048,128]{1,0:T(8,128)S(1)}, u32[]{:S(2)}, u32[]{:S(2)}) collective-permute-start(f32[2048,128]{1,0:T(8,128)S(1)} %get-tuple-element.133), channel_id=1, source_target_pairs={{0,8},{8,16},{16,24},{1,9},{9,17},{17,25},{2,10},{10,18},{18,26},{... | collective-permute-start | bytes 3145736 | tf_op jit(solution)/shard_map/ppermute | solution.py:774
  348.5 27.0 %collective-permute-start.17 = (f32[2048,128]{1,0:T(8,128)S(1)}, f32[2048,128]{1,0:T(8,128)S(1)}, u32[]{:S(2)}, u32[]{:S(2)}) collective-permute-start(f32[2048,128]{1,0:T(8,128)S(1)} %get-tuple-element.134), channel_id=1, source_target_pairs={{8,0},{16,8},{24,16},{9,1},{17,9},{25,17},{10,2},{18,10},{26,18},{... | collective-permute-start | bytes 3145736 | tf_op jit(solution)/shard_map/ppermute | solution.py:775
  377.2 24.7 %collective-permute-start.18 = (f32[2048,128]{1,0:T(8,128)}, f32[2048,128]{1,0:T(8,128)}, u32[]{:S(2)}, u32[]{:S(2)}) collective-permute-start(f32[2048,128]{1,0:T(8,128)} %get-tuple-element.137), channel_id=1, source_target_pairs={{0,8},{8,16},{16,24},{1,9},{9,17},{17,25},{2,10},{10,18},{18,26},{... | collective-permute-start | bytes 3145736 | tf_op jit(solution)/shard_map/ppermute | solution.py:774
  380.3 26.6 %collective-permute-start.19 = (f32[2048,128]{1,0:T(8,128)}, f32[2048,128]{1,0:T(8,128)}, u32[]{:S(2)}, u32[]{:S(2)}) collective-permute-start(f32[2048,128]{1,0:T(8,128)} %get-tuple-element.138), channel_id=1, source_target_pairs={{8,0},{16,8},{24,16},{9,1},{17,9},{25,17},{10,2},{18,10},{26,18},{... | collective-permute-start | bytes 3145736 | tf_op jit(solution)/shard_map/ppermute | solution.py:775
  381.6 37.6 %all-to-all-start.6 = ((f32[8,5,128,128]{3,2,1,0:T(8,128)}), f32[8,5,128,128]{3,2,1,0:T(8,128)S(1)}, u32[]{:S(2)}, u32[]{:S(2)}) async-start(f32[8,5,128,128]{3,2,1,0:T(8,128)} %column_inverse.13), calls=%async_computation.6 | async-start | bytes 5242880 | tf_op jit(solution)/shard_map/all_to_all | solution.py:797
  420.7 36.7 %all-to-all-start.7 = ((f32[8,5,128,128]{3,2,1,0:T(8,128)}), f32[8,5,128,128]{3,2,1,0:T(8,128)}, u32[]{:S(2)}, u32[]{:S(2)}) async-start(f32[8,5,128,128]{3,2,1,0:T(8,128)} %column_inverse.15), calls=%async_computation.7 | async-start | bytes 5242880 | tf_op jit(solution)/shard_map/all_to_all | solution.py:797
  (47 other events, 590.4 us)
Sparse Core Ops, SparseCore 0:
  73.9 38.4 all-reduce.1
